TPU v7x, 32 devices: a whole 2x2x4 slice. The times are simulated.
32 devices in a mesh: res: 8 (over z, y), ch: 4 (over x, core).
Axes of the slice: x: 2, y: 2, z: 4, core: 2. Of those that a mesh axis runs over, the one named last changes fastest.
Arguments:
- sequence_matrix: bfloat16 [8, 512, 256], P(None, 'res'), may hold values from -6 to 6
- couple_matrix: bfloat16 [32, 128, 4096], P('res', 'ch')
- block_target_entry: int32 [8, 4], P('res'), may hold values from 0 to 7, as said below
- block_present_flag: int32 [8, 4], P('res'), may hold values from 0 to 1, as said below
- amino_strand: int32 [512], P('res'), may hold values from 0 to 5, never falling along the last dimension, each value on 1 to 170 neighbouring positions
- sequence_scaling_factor: float32 [256], replicated, may hold values from 0.5 to 1.5
- query_key_value_matrix: bfloat16 [4, 256, 256], P(None, None, 'ch'), may hold values from -0.375 to 0.375
- focus_result_matrix: bfloat16 [256, 256], P('ch'), may hold values from -0.375 to 0.375
- strand_focus_offset: float32 [8], replicated, may hold values from -2 to 2
- couple_scaling_factor: float32 [128], P('ch'), may hold values from 0.5 to 1.5
- focus_offset_matrix: float32 [128, 8], P('ch')
- product_scaling_factor: float32 [256], replicated, may hold values from 0.5 to 1.5
- first_factor_matrix: bfloat16 [256, 32], replicated, may hold values from -0.375 to 0.375
- second_factor_matrix: bfloat16 [256, 32], P(None, 'ch'), may hold values from -0.375 to 0.375
- product_result_matrix: bfloat16 [128, 32, 32], P(None, None, 'ch'), may hold values from -0.8984375 to 0.8984375
- product_result_offset: float32 [128], P('ch'), may hold values from -3 to 3
Outputs:
- sequence_result_matrix: bfloat16 [8, 512, 256], P(None, 'res')
- pairwise_output: bfloat16 [32, 128, 4096], P('res', 'ch')
Inputs may be any that keep to these rules, and one draw needn't show every extreme that they name: `block_target_entry`: slot 0 of row tile r names r itself; the column tiles of one row tile are distinct. `block_present_flag`: the valid slots of each row tile are its first ones, two or more of them; in every draw some row tile has all 4 slots valid.
All inputs are finite; a program needn't handle non-finite values.
Results may differ from a plain program's by a relative error of at most 0.005.
Values may be sent and summed in bfloat16 or wider, within the bound.
No kernel may reach another device: no remote copies, remote signals or barrier semaphores. Data moves between devices by JAX's collectives and lax.ppermute only.
A program may use at most 128 MiB of HBM per device.

v0:
```python
import math

import jax
import jax.numpy as jnp
from jax import lax
from jax.sharding import PartitionSpec as P

C_Z = 128
FOCUS_NUMBER = 8
FOCUS_BREADTH = 32
PRODUCT_FEATURE = 32


EPS = 1e-05
MASKED = -1e30


def final_dimension_standardize(values, gain_vector):
    values = values.astype(jnp.float32)
    average = jnp.mean(values, axis=-1, keepdims=True)
    variance = jnp.mean(jnp.square(values - average), axis=-1, keepdims=True)
    return (values - average) * lax.rsqrt(variance + EPS) * gain_vector


def on_device(
    sequence_matrix,
    couple_matrix,
    block_target_entry,
    block_present_flag,
    amino_strand,
    sequence_scaling_factor,
    query_key_value_matrix,
    focus_result_matrix,
    strand_focus_offset,
    couple_scaling_factor,
    focus_offset_matrix,
    product_scaling_factor,
    first_factor_matrix,
    second_factor_matrix,
    product_result_matrix,
    product_result_offset,
):
    groups = lax.axis_size("ch")
    group_index = lax.axis_index("ch")
    local_heads = FOCUS_NUMBER // groups
    slot_count = couple_matrix.shape[0]
    cell_count = couple_matrix.shape[2]
    block_extent = sequence_matrix.shape[1]
    sequence_number_overall = sequence_matrix.shape[0]
    pair_field = couple_matrix.astype(jnp.float32)
    part_one = jnp.sum(pair_field, axis=1)
    part_two = jnp.sum(pair_field * pair_field, axis=1)
    sum_one, sum_two = lax.psum((part_one, part_two), "ch")
    center = sum_one / C_Z
    spread = lax.rsqrt(sum_two / C_Z - center * center + EPS)
    normed = (
        (pair_field - center[:, None, :])
        * spread[:, None, :]
        * couple_scaling_factor[None, :, None]
    )
    partial_value = jnp.einsum(
        "kcp,ch->hkp", normed, focus_offset_matrix, precision=lax.Precision.HIGHEST
    )
    head_bias = lax.psum_scatter(partial_value, "ch", scatter_dimension=0, tiled=True)
    head_bias = head_bias.astype(jnp.bfloat16)
    bias_all, cols_all, valid_all, chain_all = (
        lax.all_gather(head_bias, "res", axis=1, tiled=True),
        lax.all_gather(block_target_entry, "res", axis=0, tiled=True),
        lax.all_gather(block_present_flag, "res", axis=0, tiled=True),
        lax.all_gather(amino_strand, "res", axis=0, tiled=True),
    )
    sequence_first_layout = lax.all_to_all(
        sequence_matrix, "res", split_axis=0, concat_axis=1, tiled=True
    )
    device_rows, amino_number_here, sequence_feature_breadth = sequence_first_layout.shape
    tile_count = amino_number_here // block_extent
    sequence_standardized = final_dimension_standardize(
        sequence_first_layout, sequence_scaling_factor
    ).astype(jnp.bfloat16)
    projected_rows = jnp.einsum(
        "hbx,sxt->shbt",
        sequence_standardized,
        query_key_value_matrix,
        preferred_element_type=jnp.float32,
    ).astype(jnp.bfloat16)
    projected_rows = projected_rows.reshape(
        4, device_rows, tile_count, block_extent, local_heads, FOCUS_BREADTH
    )
    queries = projected_rows[0]
    keyset = projected_rows[1]
    valueset = projected_rows[2]
    gateset = projected_rows[3]
    chain_tiles = chain_all.reshape(tile_count, block_extent)
    bias_tiles = bias_all.reshape(local_heads, tile_count, slot_count, block_extent, block_extent)
    head_scale = lax.dynamic_slice_in_dim(
        strand_focus_offset, group_index * local_heads, local_heads, 0
    )
    block_tiles = math.gcd(tile_count, max(1, 512 // block_extent))

    def attend(block_index):
        first_tile = block_index * block_tiles
        columns = lax.dynamic_slice_in_dim(cols_all, first_tile, block_tiles, 0)
        usable = lax.dynamic_slice_in_dim(valid_all, first_tile, block_tiles, 0) > 0
        query_block = lax.dynamic_slice_in_dim(queries, first_tile, block_tiles, 1)
        key_block = keyset[:, columns]
        value_block = valueset[:, columns]
        scores = jnp.einsum(
            "rgahd,rgkbhd->rghakb", query_block, key_block, preferred_element_type=jnp.float32
        ) * FOCUS_BREADTH ** (-0.5)
        pair_part = lax.dynamic_slice_in_dim(bias_tiles, first_tile, block_tiles, 1).astype(
            jnp.float32
        )
        pair_part = pair_part.transpose(1, 0, 3, 2, 4)
        query_chain = lax.dynamic_slice_in_dim(chain_tiles, first_tile, block_tiles, 0)
        same_chain = (query_chain[:, :, None, None] == chain_tiles[columns][:, None, :, :]).astype(
            jnp.float32
        )
        scores = (
            scores
            + pair_part[None]
            + head_scale[None, None, :, None, None, None] * same_chain[None, :, None]
        )
        scores = jnp.where(usable[None, :, None, None, :, None], scores, MASKED)
        row_max = jnp.max(scores, axis=(4, 5), keepdims=True)
        exponent = jnp.exp(scores - row_max)
        attn_weights = (exponent / jnp.sum(exponent, axis=(4, 5), keepdims=True)).astype(
            jnp.bfloat16
        )
        mixed = jnp.einsum(
            "rghakb,rgkbhd->rgahd", attn_weights, value_block, preferred_element_type=jnp.float32
        )
        gate_block = lax.dynamic_slice_in_dim(gateset, first_tile, block_tiles, 1).astype(
            jnp.float32
        )
        return (mixed * jax.nn.sigmoid(gate_block)).astype(jnp.bfloat16)

    blocks = lax.map(attend, jnp.arange(tile_count // block_tiles, dtype=jnp.int32))
    attended_rows = blocks.transpose(1, 0, 2, 3, 4, 5).reshape(
        device_rows * amino_number_here, local_heads * FOCUS_BREADTH
    )
    residual_input = sequence_first_layout.reshape(
        device_rows * amino_number_here, sequence_feature_breadth
    )
    partial_out = jnp.dot(attended_rows, focus_result_matrix, preferred_element_type=jnp.float32)
    head_total = lax.psum(partial_out, "ch")
    updated_state = (
        (residual_input.astype(jnp.float32) + head_total)
        .astype(jnp.bfloat16)
        .reshape(device_rows, amino_number_here, sequence_feature_breadth)
    )
    sequence_result_matrix = lax.all_to_all(
        updated_state, "res", split_axis=1, concat_axis=0, tiled=True
    )
    outer_normed = (
        final_dimension_standardize(sequence_result_matrix, product_scaling_factor)
        .astype(jnp.bfloat16)
        .reshape(sequence_number_overall * block_extent, sequence_feature_breadth)
    )
    left_projected = (
        jnp.dot(outer_normed, first_factor_matrix, preferred_element_type=jnp.float32)
        .astype(jnp.bfloat16)
        .reshape(sequence_number_overall, block_extent * PRODUCT_FEATURE)
    )
    own_columns = block_target_entry[0]
    right_projected = (
        jnp.dot(outer_normed, second_factor_matrix, preferred_element_type=jnp.float32)
        .astype(jnp.bfloat16)
        .reshape(sequence_number_overall, block_extent, -1)
    )
    narrow = right_projected.shape[2]
    weight_flat = product_result_matrix.reshape(C_Z, PRODUCT_FEATURE * narrow)
    empty_tiles = jnp.zeros(
        (slot_count, sequence_number_overall, block_extent, narrow), jnp.bfloat16
    )
    shard_piece = lax.all_gather(right_projected, "res", axis=1, tiled=True)
    piece_rows = shard_piece.shape[1]
    offset = own_columns * block_extent
    inside = (offset >= 0) & (offset < piece_rows)

    def take_one(offset_one, inside_one, held_tile):
        taken = lax.dynamic_slice_in_dim(
            shard_piece, jnp.clip(offset_one, 0, piece_rows - block_extent), block_extent, 1
        )
        return jnp.where(inside_one, taken, held_tile)

    chosen = jax.vmap(take_one, in_axes=(0, 0, 0))(offset, inside, empty_tiles)
    left_turned = left_projected.T

    def outer_one(right_tile_rows):
        product = (
            jnp.dot(
                left_turned,
                right_tile_rows.reshape(sequence_number_overall, block_extent * narrow),
                preferred_element_type=jnp.float32,
            )
            / sequence_number_overall
        )
        product = (
            product.reshape(block_extent, PRODUCT_FEATURE, block_extent, narrow)
            .transpose(1, 3, 0, 2)
            .astype(jnp.bfloat16)
            .reshape(PRODUCT_FEATURE * narrow, cell_count)
        )
        return jnp.dot(weight_flat, product, preferred_element_type=jnp.float32)

    partials = lax.map(outer_one, chosen)
    summed = lax.psum_scatter(partials, "ch", scatter_dimension=1, tiled=True)
    keep_mask = block_present_flag[0].astype(jnp.float32)
    pairwise_output = (
        pair_field + keep_mask[:, None, None] * (summed + product_result_offset[None, :, None])
    ).astype(jnp.bfloat16)
    return (sequence_result_matrix, pairwise_output)


def solution(mesh):
    return jax.shard_map(
        on_device,
        mesh=mesh,
        in_specs=(
            P(None, "res", None),
            P("res", "ch", None),
            P("res", None),
            P("res", None),
            P("res"),
            P(),
            P(None, None, "ch"),
            P("ch", None),
            P(),
            P("ch"),
            P("ch", None),
            P(),
            P(),
            P(None, "ch"),
            P(None, None, "ch"),
            P("ch"),
        ),
        out_specs=(P(None, "res", None), P("res", "ch", None)),
        check_vma=False,
    )
```

profile of v0, /device:TPU:0, one launch (start us, length us, event | category | flops | bytes accessed | tf_op | source)
XLA Modules:
  0.0 450.4 jit_solution(9530738559762649015)
XLA Ops:
  7.2 7.5 %all-to-all-start = ((bf16[8,64,256]{2,1,0:T(8,128)(2,1)}), bf16[8,64,256]{2,1,0:T(8,128)(2,1)S(1)}, u32[]{:S(2)}, u32[]{:S(2)}) async-start(bf16[8,64,256]{2,1,0:T(8,128)(2,1)} %param.18), calls=%async_computation | async-start | bytes 524288 | tf_op jit(solution)/shard_map/all_to_all | solution.py:72
  14.7 2.4 convert_reduce_fusion
  17.2 1.2 dynamic-slice
  20.0 11.8 %all-reduce = s32[512]{0:T(512)S(1)} all-reduce(s32[512]{0:T(512)S(1)} %dynamic-update-slice), channel_id=1, replica_groups=mesh['res'=8,'ch'=4] {'res'}, use_global_device_ids=true, to_apply=%add | all-reduce | flops 512 | bytes 4096
  31.9 17.9 %all-gather = s32[8,1,4]{2,1,0:T(1,128)S(1)} all-gather(s32[1,1,4]{2,1,0:T(1,128)} %bitcast.164), channel_id=1, replica_groups=mesh['res'=8,'ch'=4] {'res'}, dimensions={0}, use_global_device_ids=true | all-gather | bytes 144 | tf_op jit(solution)/shard_map/all_gather | solution.py:68
  50.6 1.3 compare_convert_fusion
  51.9 16.8 %all-gather.1 = s32[8,1,4]{2,1,0:T(1,128)S(1)} all-gather(s32[1,1,4]{2,1,0:T(1,128)S(1)} %bitcast.165), channel_id=1, replica_groups=mesh['res'=8,'ch'=4] {'res'}, dimensions={0}, use_global_device_ids=true | all-gather | bytes 144 | tf_op jit(solution)/shard_map/all_gather | solution.py:69
  71.2 1.5 convolution_bitcast_fusion.1
  73.0 16.4 %all-reduce.10 = bf16[8,4,4096]{2,1,0:T(4,128)(2,1)S(1)} all-reduce(f32[8,4,4096]{2,1,0:T(4,128)S(1)} %copy.104), channel_id=2, replica_groups=mesh['res'=8,'ch'=4] {'ch'}, use_global_device_ids=true, to_apply=%region_6.0.clone | all-reduce | flops 131072 | bytes 786432
  89.5 31.4 %all_gather.17 = bf16[2,32,4096]{2,0,1:T(2,128)(2,1)S(1)} all-gather(bf16[2,4,4096]{2,0,1:T(2,128)(2,1)S(1)} %copy.105), channel_id=1, replica_groups=mesh['res'=8,'ch'=4] {'res'}, dimensions={1}, use_global_device_ids=true | all-gather | bytes 589824 | tf_op jit(solution)/shard_map/all_gather | solution.py:67
  121.3 2.2 reshape.314
  123.5 1.9 copy.107
  129.1 1.4 gather_fusion
  131.3 2.1 fusion.31
  136.4 31.8 %all-reduce.7.cloned.1.call-done = f32[512,256]{1,0:T(8,128)} async-done(((f32[512,256]{1,0:T(8,128)}), f32[512,256]{1,0:T(8,128)}) %all-reduce.7.cloned.1.call-update) | async-done | bytes 524304 | tf_op jit(solution)/shard_map/psum | solution.py:145
  170.2 2.2 reduce.8
  173.2 5.6 %all-to-all-start.1 = ((bf16[8,2,8192]{2,1,0:T(2,128)(2,1)}), bf16[8,2,8192]{2,1,0:T(2,128)(2,1)S(1)}, u32[]{:S(2)}, u32[]{:S(2)}) async-start(bf16[8,2,8192]{2,1,0:T(2,128)(2,1)} %reshape.378), calls=%async_computation.1 | async-start | bytes 524288 | tf_op jit(solution)/shard_map/all_to_all | solution.py:151
  179.1 8.0 %all-to-all-done.1 = bf16[8,2,8192]{2,1,0:T(2,128)(2,1)S(1)} async-done(((bf16[8,2,8192]{2,1,0:T(2,128)(2,1)}), bf16[8,2,8192]{2,1,0:T(2,128)(2,1)S(1)}, u32[]{:S(2)}, u32[]{:S(2)}) %all-to-all-start.1) | async-done | bytes 262176 | tf_op jit(solution)/shard_map/all_to_all | solution.py:151
  187.9 1.3 convert_reduce_fusion.2
  189.2 7.4 %multiply_reduce_fusion = f32[512]{0:T(512)S(1)} fusion(f32[512]{0:T(512)S(1)} %broadcast_multiply_fusion.2, bf16[512,1,256]{2,1,0:T(2,128)(2,1)S(1)} %reshape.379), kind=kLoop, calls=%fused_computation.49 | loop fusion | flops 523776 | bytes 266240 | tf_op jit(solution)/shard_map/reduce_sum | solution.py:21
  197.2 33.1 %all_gather.19 = bf16[8,512,8]{2,0,1:T(8,128)(2,1)S(1)} all-gather(bf16[8,64,8]{2,0,1:T(8,128)(2,1)S(1)} %copy.113), channel_id=1, replica_groups=mesh['res'=8,'ch'=4] {'res'}, dimensions={1}, use_global_device_ids=true | all-gather | bytes 73728 | tf_op jit(solution)/shard_map/all_gather | solution.py:175
  231.6 139.8 %while.2 = (s32[]{:T(128)}, f32[4,128,4096]{2,1,0:T(8,128)}, bf16[4,8,64,8]{3,1,2,0:T(8,128)(2,1)S(1)}, bf16[2048,8]{0,1:T(8,128)(2,1)S(1)}, bf16[128,256]{1,0:T(8,128)(2,1)S(1)}, /*index=5*/s32[]{:T(128)}) while((s32[]{:T(128)}, f32[4,128,4096]{2,1,0:T(8,128)}, bf16[4,8,64,8]{3,1,2,0:T(8,128)(2,1)S(1)}, bf16[2048,8]{0,1:T(8,128)(2,1)S(1)}, ...), condition=%wide.region_13.14_spmd, body=%wide.region_12.13_spmd.sunk | while | flops 287309824 | bytes 27418708 | solution.py:206
  232.6 8.1 %convert_element_type.203 = bf16[64,32,64,8]{1,0,3,2:T(8,128)(2,1)} reshape(bf16[2048,512]{0,1:T(8,128)(2,1)S(1)} %fusion.55) | data formatting | bytes 4194304 | tf_op jit(solution)/shard_map/while/body/eval_jaxpr/convert_element_type | solution.py:201
  240.7 14.6 %copy.154 = bf16[32,8,64,64]{3,2,1,0:T(8,128)(2,1)} copy(bf16[32,8,64,64]{0,2,1,3:T(8,128)(2,1)} %bitcast.151) | data formatting | bytes 4194304 | tf_op jit(solution)/shard_map/while/body/eval_jaxpr/convert_element_type | solution.py:201
  255.3 5.7 %reshape.383 = bf16[256,4096]{1,0:T(8,128)(2,1)S(1)} reshape(bf16[32,8,64,64]{3,2,1,0:T(8,128)(2,1)} %copy.154) | data formatting | bytes 4194304 | tf_op jit(solution)/shard_map/while/body/eval_jaxpr/reshape | solution.py:202
  261.0 2.2 convolution_bitcast_fusion.4
  263.1 1.9 copy.155
  265.1 1.5 constant_dynamic-update-slice_fusion.2
  267.6 8.1 %convert_element_type.203 = bf16[64,32,64,8]{1,0,3,2:T(8,128)(2,1)} reshape(bf16[2048,512]{0,1:T(8,128)(2,1)S(1)} %fusion.55) | data formatting | bytes 4194304 | tf_op jit(solution)/shard_map/while/body/eval_jaxpr/convert_element_type | solution.py:201
  275.7 14.6 %copy.154 = bf16[32,8,64,64]{3,2,1,0:T(8,128)(2,1)} copy(bf16[32,8,64,64]{0,2,1,3:T(8,128)(2,1)} %bitcast.151) | data formatting | bytes 4194304 | tf_op jit(solution)/shard_map/while/body/eval_jaxpr/convert_element_type | solution.py:201
  290.3 5.7 %reshape.383 = bf16[256,4096]{1,0:T(8,128)(2,1)S(1)} reshape(bf16[32,8,64,64]{3,2,1,0:T(8,128)(2,1)} %copy.154) | data formatting | bytes 4194304 | tf_op jit(solution)/shard_map/while/body/eval_jaxpr/reshape | solution.py:202
  296.0 2.2 convolution_bitcast_fusion.4
  298.1 1.9 copy.155
  300.1 1.4 constant_dynamic-update-slice_fusion.2
  302.5 8.1 %convert_element_type.203 = bf16[64,32,64,8]{1,0,3,2:T(8,128)(2,1)} reshape(bf16[2048,512]{0,1:T(8,128)(2,1)S(1)} %fusion.55) | data formatting | bytes 4194304 | tf_op jit(solution)/shard_map/while/body/eval_jaxpr/convert_element_type | solution.py:201
  310.6 14.6 %copy.154 = bf16[32,8,64,64]{3,2,1,0:T(8,128)(2,1)} copy(bf16[32,8,64,64]{0,2,1,3:T(8,128)(2,1)} %bitcast.151) | data formatting | bytes 4194304 | tf_op jit(solution)/shard_map/while/body/eval_jaxpr/convert_element_type | solution.py:201
  325.2 5.7 %reshape.383 = bf16[256,4096]{1,0:T(8,128)(2,1)S(1)} reshape(bf16[32,8,64,64]{3,2,1,0:T(8,128)(2,1)} %copy.154) | data formatting | bytes 4194304 | tf_op jit(solution)/shard_map/while/body/eval_jaxpr/reshape | solution.py:202
  330.9 2.2 convolution_bitcast_fusion.4
  333.0 1.9 copy.155
  335.0 1.5 constant_dynamic-update-slice_fusion.2
  337.4 8.1 %convert_element_type.203 = bf16[64,32,64,8]{1,0,3,2:T(8,128)(2,1)} reshape(bf16[2048,512]{0,1:T(8,128)(2,1)S(1)} %fusion.55) | data formatting | bytes 4194304 | tf_op jit(solution)/shard_map/while/body/eval_jaxpr/convert_element_type | solution.py:201
  345.6 14.6 %copy.154 = bf16[32,8,64,64]{3,2,1,0:T(8,128)(2,1)} copy(bf16[32,8,64,64]{0,2,1,3:T(8,128)(2,1)} %bitcast.151) | data formatting | bytes 4194304 | tf_op jit(solution)/shard_map/while/body/eval_jaxpr/convert_element_type | solution.py:201
  360.2 5.7 %reshape.383 = bf16[256,4096]{1,0:T(8,128)(2,1)S(1)} reshape(bf16[32,8,64,64]{3,2,1,0:T(8,128)(2,1)} %copy.154) | data formatting | bytes 4194304 | tf_op jit(solution)/shard_map/while/body/eval_jaxpr/reshape | solution.py:202
  365.8 2.2 convolution_bitcast_fusion.4
  368.0 1.9 copy.155
  369.9 1.5 constant_dynamic-update-slice_fusion.2
  372.2 68.8 %reduce-scatter.2.cloned.1.call-done = f32[4,32,4096]{2,1,0:T(8,128)} async-done(((f32[4,128,4096]{2,1,0:T(8,128)}), f32[4,32,4096]{2,1,0:T(8,128)}) %reduce-scatter.2.cloned.1.call-update) | async-done | bytes 2097168 | tf_op jit(solution)/shard_map/reduce_scatter | solution.py:207
  441.0 3.0 fusion.5
  (125 shorter events, 22.2 us)
Async XLA Ops:
  7.2 119.0 %copy-start = (bf16[4,256,64]{1,2,0:T(8,128)(2,1)S(1)}, bf16[4,256,64]{1,2,0:T(8,128)(2,1)}, u32[]{:S(2)}) copy-start(bf16[4,256,64]{1,2,0:T(8,128)(2,1)} %param.24) | copy-start | bytes 393220
  7.2 61.8 %copy-start.17 = (u32[32]{0:T(128)S(1)}, u32[32]{0:T(128)}, u32[]{:S(2)}) copy-start(u32[32]{0:T(128)} %constant.112) | copy-start | bytes 388
  7.2 64.0 %copy-start.1 = (bf16[4,32,4096]{2,1,0:T(8,128)(2,1)S(1)}, bf16[4,32,4096]{2,1,0:T(8,128)(2,1)}, u32[]{:S(2)}) copy-start(bf16[4,32,4096]{2,1,0:T(8,128)(2,1)} %param.19) | copy-start | bytes 3145732
  7.2 44.7 %copy-start.13 = (s32[1,4]{1,0:T(1,128)S(1)}, s32[1,4]{1,0:T(1,128)}, u32[]{:S(2)}) copy-start(s32[1,4]{1,0:T(1,128)} %param.21) | copy-start | bytes 52
  7.2 61.7 %copy-start.15 = (f32[8]{0:T(128)S(1)}, f32[8]{0:T(128)}, u32[]{:S(2)}) copy-start(f32[8]{0:T(128)} %param.26) | copy-start | bytes 100
  7.2 64.0 %copy-start.16 = (f32[32]{0:T(128)S(1)}, f32[32]{0:T(128)}, u32[]{:S(2)}) copy-start(f32[32]{0:T(128)} %param.27) | copy-start | bytes 388
  7.2 64.0 %copy-start.14 = (f32[32,8]{0,1:T(8,128)S(1)}, f32[32,8]{0,1:T(8,128)}, u32[]{:S(2)}) copy-start(f32[32,8]{0,1:T(8,128)} %param.28) | copy-start | bytes 3076
  7.2 118.2 %all-to-all-start = ((bf16[8,64,256]{2,1,0:T(8,128)(2,1)}), bf16[8,64,256]{2,1,0:T(8,128)(2,1)S(1)}, u32[]{:S(2)}, u32[]{:S(2)}) async-start(bf16[8,64,256]{2,1,0:T(8,128)(2,1)} %param.18), calls=%async_computation | async-start | bytes 524288 | tf_op jit(solution)/shard_map/all_to_all | solution.py:72
  14.7 55.5 %all-reduce.9.cloned.1.call-start = ((), (), s32[]{:S(2)}) async-start(), calls=%async_computation.5 | async-start | bytes 262144 | tf_op jit(solution)/shard_map/psum | solution.py:53
  17.1 151.0 %all-reduce.7.cloned.1.call-start = ((), (), s32[]{:S(2)}) async-start(), calls=%async_computation.3 | async-start | bytes 1048576 | tf_op jit(solution)/shard_map/psum | solution.py:145
  123.5 2.5 copy-start.9
  133.4 1.0 copy-start.3
  133.4 1.1 copy-start.4
  134.5 0.8 copy-start.6
  136.3 42.6 %copy-start.5 = (bf16[128,32,8]{0,2,1:T(8,128)(2,1)S(1)}, bf16[128,32,8]{0,2,1:T(8,128)(2,1)}, u32[]{:S(2)}) copy-start(bf16[128,32,8]{0,2,1:T(8,128)(2,1)} %param.32) | copy-start | bytes 196612
  136.3 42.7 %copy-start.12 = (s32[1,4]{1,0:T(1,128)S(1)}, s32[1,4]{1,0:T(1,128)}, u32[]{:S(2)}) copy-start(s32[1,4]{1,0:T(1,128)} %param.20) | copy-start | bytes 52
  172.4 24.2 %copy-start.10 = (f32[256]{0:T(256)S(1)}, f32[256]{0:T(256)}, u32[]{:S(2)}) copy-start(f32[256]{0:T(256)} %param.29) | copy-start | bytes 3076
  173.2 23.6 %copy-start.8 = (bf16[256,8]{0,1:T(8,128)(2,1)S(1)}, bf16[256,8]{0,1:T(8,128)(2,1)}, u32[]{:S(2)}) copy-start(bf16[256,8]{0,1:T(8,128)(2,1)} %param.31) | copy-start | bytes 12292
  173.2 13.9 %all-to-all-start.1 = ((bf16[8,2,8192]{2,1,0:T(2,128)(2,1)}), bf16[8,2,8192]{2,1,0:T(2,128)(2,1)S(1)}, u32[]{:S(2)}, u32[]{:S(2)}) async-start(bf16[8,2,8192]{2,1,0:T(2,128)(2,1)} %reshape.378), calls=%async_computation.1 | async-start | bytes 524288 | tf_op jit(solution)/shard_map/all_to_all | solution.py:151
  178.8 262.1 %reduce-scatter.2.cloned.1.call-start = ((), (), s32[]{:S(2)}) async-start(), calls=%async_computation.4 | async-start | bytes 10485760 | tf_op jit(solution)/shard_map/reduce_scatter | solution.py:207
  187.3 43.0 %copy-start.7 = (bf16[256,32]{0,1:T(8,128)(2,1)S(1)}, bf16[256,32]{0,1:T(8,128)(2,1)}, u32[]{:S(2)}) copy-start(bf16[256,32]{0,1:T(8,128)(2,1)} %param.30) | copy-start | bytes 49156
  371.4 69.5 %copy-start.2 = (bf16[4,32,4096]{2,1,0:T(8,128)(2,1)S(1)}, bf16[4,32,4096]{2,1,0:T(8,128)(2,1)}, u32[]{:S(2)}) copy-start(bf16[4,32,4096]{2,1,0:T(8,128)(2,1)} %param.19) | copy-start | bytes 3145732
  371.4 69.5 %copy-start.11 = (f32[32]{0:T(128)S(1)}, f32[32]{0:T(128)}, u32[]{:S(2)}) copy-start(f32[32]{0:T(128)} %param.33) | copy-start | bytes 388
Sparse Core Ops, SparseCore 0:
  18.5 33.1 all-reduce.8
  136.5 31.6 all-reduce.6
  371.6 69.3 reduce-scatter.1
where the time goes:
time: 452 us; the launch traced here: 450 us
  local copies, waits for them, and re-layouts  146 us (32%)
  blocking collectives  127 us (28%)
  waiting for transfers between devices  109 us (24%)
  other arithmetic  21.8 us (5%)
  matrix products  17.3 us (4%)
  between operations  15.5 us (3%)
  starting transfers between devices  13.2 us (3%)
    convert_element_type x8, local copies, waits for them, and re-layouts, outer_one(): product = product.reshape(block_extent, PRODUCT_FEATURE, block_extent, na...  90.9 us
    reduce_scatter x1, waiting for transfers between devices, on_device(): summed = lax.psum_scatter(partials, 'ch', scatter_dimension=1, tiled=True)  68.8 us
    all_gather x1, blocking collectives, on_device(): shard_piece = lax.all_gather(right_projected, 'res', axis=1, tiled=True)  33.1 us
    psum x1, waiting for transfers between devices, on_device(): head_total = lax.psum(partial_out, 'ch')  31.8 us
    all_gather x1, blocking collectives, on_device(): lax.all_gather(head_bias, 'res', axis=1, tiled=True)  31.4 us
    unnamed x2, blocking collectives  28.2 us
    reshape x4, local copies, waits for them, and re-layouts, outer_one(): product = product.reshape(block_extent, PRODUCT_FEATURE, block_extent, na...  22.7 us
    all_gather x1, blocking collectives, on_device(): lax.all_gather(block_target_entry, 'res', axis=0, tiled=True)  17.9 us
  transfers between devices with their start and end apart: 5, of which 3 were waited for; matrix products, arithmetic and copies ran while one was open for 4% of the time, Pallas kernels for 0%

commit v1 on v0

--- a/solution.py
+++ b/solution.py
@@ -1,9 +1,13 @@
+import functools
 import math
 
 import jax
 import jax.numpy as jnp
 from jax import lax
+from jax.experimental import pallas as pl
+from jax.experimental.pallas import tpu as pltpu
 from jax.sharding import PartitionSpec as P
+
 
 C_Z = 128
 FOCUS_NUMBER = 8
@@ -212,9 +216,766 @@
     return (sequence_result_matrix, pairwise_output)
 
 
+ACROSS = (((1,), (0,)), ((), ()))
+BOTH_LAST = (((1,), (1,)), ((), ()))
+VMEM_LIMIT = 12 * 1024 * 1024
+
+
+def flip(values, axis, bits):
+    size = lax.axis_size(axis)
+    return lax.ppermute(values, axis, [(i, i ^ bits) for i in range(size)])
+
+
+def over_groups(values, relay):
+    across = flip(values, "ch", 2)
+    near = flip(values, "ch", 1)
+    if relay:
+        far = flip(across, "ch", 1)
+    else:
+        far = flip(values, "ch", 3)
+    return [values, near, across, far]
+
+
+def over_tiles(values):
+    size = lax.axis_size("res")
+    found = {0: values}
+    for bits in range(size - 2, 0, -2):
+        found[bits] = flip(values, "res", bits)
+    for bits in range(0, size, 2):
+        found[bits + 1] = flip(found[bits], "res", 1)
+    return [found[bits] for bits in range(size)]
+
+
+def dot(a, b, dims):
+    return lax.dot_general(a, b, dims, preferred_element_type=jnp.float32)
+
+
+def lane_block(shape, width):
+    return lax.broadcasted_iota(jnp.int32, shape, len(shape) - 1) // width
+
+
+def standardized(values, gain):
+    average = jnp.mean(values, axis=-1, keepdims=True)
+    centred = values - average
+    variance = jnp.mean(centred * centred, axis=-1, keepdims=True)
+    return centred * lax.rsqrt(variance + EPS) * gain
+
+
+def put(ref, values):
+    for b in range(ref.shape[0]):
+        ref[b] = values[:, b * 128 : (b + 1) * 128]
+
+
+def take(ref):
+    return jnp.concatenate([ref[b] for b in range(ref.shape[0])], axis=1)
+
+
+def put_every(ref, start, step, values, first=0):
+    for b in range(values.shape[1] // 128):
+        ref[first + b, pl.ds(start, values.shape[0], stride=step), :] = values[
+            :, b * 128 : (b + 1) * 128
+        ]
+
+
+def take_every(ref, start, size, step):
+    return jnp.concatenate(
+        [ref[b, pl.ds(start, size, stride=step), :] for b in range(ref.shape[0])], axis=1
+    )
+
+
+def spec():
+    return pl.BlockSpec(memory_space=pltpu.VMEM)
+
+
+def call(body, out, inputs, specs, scratch, flops, moved):
+    out_specs = jax.tree.map(lambda _: spec(), out)
+    return pl.pallas_call(
+        body,
+        out_shape=out,
+        in_specs=specs,
+        out_specs=out_specs,
+        scratch_shapes=scratch,
+        cost_estimate=pl.CostEstimate(flops=flops, bytes_accessed=moved, transcendentals=0),
+        compiler_params=pltpu.CompilerParams(vmem_limit_bytes=VMEM_LIMIT),
+    )(*inputs)
+
+
+def column(row, lanes):
+    return jnp.broadcast_to(row, (lanes, row.shape[1])).T
+
+
+def prepare(extent, rows, *refs):
+    sources, outs, scratch = refs[:16], refs[16:28], refs[28:]
+    sequence, pair, query_key_value, out_weight, second, strand = sources[:6]
+    gain_pair, focus, gain_one, gain_two, first, offset, chain_gain = sources[6:13]
+    product, target, present = sources[13:]
+    tile_ref, weight_ref, pair_ref, sum_weight_ref, gain_one_ref, gain_two_ref = outs[:6]
+    first_ref, offset_ref, chain_ref, chain_gain_ref, place_ref, open_ref = outs[6:]
+    held_second, held_strand, held_gain, held_focus, held_first, held_offset = scratch[:6]
+    held_chain_gain, held_target, held_present, wide, tall, sems = scratch[6:]
+    lines = rows * extent
+    group = lax.axis_index("ch")
+    narrow = second.shape[0]
+    moves = [
+        (strand, held_strand),
+        (second, held_second),
+        (gain_pair, held_gain),
+        (focus, held_focus),
+        (first, held_first),
+        (offset, held_offset),
+        (chain_gain, held_chain_gain),
+        (target, held_target),
+        (present, held_present),
+        (gain_one, gain_one_ref),
+        (gain_two, gain_two_ref),
+        (out_weight, weight_ref.at[4]),
+        (query_key_value, weight_ref.at[0:4]),
+        (pair, pair_ref),
+    ]
+    deep = weight_ref.shape[1]
+    for i in range(product.shape[0] // deep):
+        part = pl.ds((i % 2) * 128, 128)
+        moves.append(
+            (product.at[pl.ds(i * deep, deep)], weight_ref.at[6 + i // 2, :, part])
+        )
+    for s in range(rows):
+        moves.append(
+            (sequence.at[group * rows + s], tile_ref.at[s * extent : (s + 1) * extent])
+        )
+    copies = [
+        pltpu.make_async_copy(source, target, sems.at[i])
+        for i, (source, target) in enumerate(moves)
+    ]
+    for copy in copies:
+        copy.start()
+    for copy in copies[:9]:
+        copy.wait()
+    width = tile_ref.shape[1]
+    tile = lax.axis_index("res")
+    slots = target.shape[1]
+    for k in range(slots):
+        place_ref[k : k + 1, :] = jnp.full((1, 128), held_target[0, k] ^ tile)
+        open_ref[k : k + 1, :] = jnp.full((1, 128), held_present[0, k]).astype(jnp.float32)
+    chain = held_strand[...].astype(jnp.float32)
+    twice = jnp.concatenate([chain] * (128 // extent), axis=1)
+    line = jnp.broadcast_to(jnp.concatenate([twice] * (width // 128), axis=1), (8, width))
+    tile_ref[lines:, :] = line.astype(jnp.bfloat16)
+    tall[...] = column(chain, 128)
+    half = extent // 2
+    for p in range(2):
+        chain_ref[p * half : (p + 1) * half, :] = tall[pl.ds(p, half, stride=2), :]
+    spread = lax.broadcasted_iota(jnp.int32, (weight_ref.shape[1], width), 0)
+    factor = jnp.concatenate(
+        [held_second[...].astype(jnp.float32)] * (weight_ref.shape[1] // narrow), axis=0
+    )
+    weight_ref[5] = jnp.where(spread // narrow == group, factor, 0.0).astype(jnp.bfloat16)
+    gains = held_focus[...] * held_gain[...]
+    one = gains.astype(jnp.bfloat16).astype(jnp.float32)
+    two = (gains - one).astype(jnp.bfloat16).astype(jnp.float32)
+    sum_weight_ref[...] = jnp.concatenate(
+        [one, two, gains - one - two, jnp.ones_like(gains)], axis=0
+    ).astype(jnp.bfloat16)
+    put(wide, held_first[...].astype(jnp.float32))
+    features = first_ref.shape[0]
+    first_ref[...] = jnp.concatenate(
+        [take_every(wide, i, features // 4, 4) for i in range(4)], axis=0
+    ).astype(jnp.bfloat16)
+    offset_ref[...] = column(held_offset[...], 128)
+    chain_gain_ref[...] = column(held_chain_gain[...], 128)
+    for copy in copies[9:]:
+        copy.wait()
+
+
+def pair_sums(keep, weight_ref, pair_ref, out_ref):
+    slots = pair_ref.shape[0] // 2
+    channels, cells = pair_ref.shape[1:]
+    odd = lax.rem(lax.axis_index("ch"), 2)
+    half = odd if keep else 1 - odd
+    weights = weight_ref[...]
+    heads = FOCUS_NUMBER
+    pieces = heads // 2
+    stretch = cells // pieces
+    total = jnp.sum(weights.astype(jnp.float32), axis=1, keepdims=True)
+    gain = total[0:heads] + total[heads : 2 * heads] + total[2 * heads : 3 * heads]
+    step = 512
+    for k in range(slots):
+        slot = half * slots + k
+        for start in range(0, cells, step):
+            part = pl.ds(start, step)
+            block = pair_ref[slot, :, part]
+            sums = dot(weights, block, ACROSS)
+            mean = sums[3 * heads : 3 * heads + 1] * (1.0 / channels)
+            head = sums[0:heads] + sums[heads : 2 * heads] + sums[2 * heads : 3 * heads]
+            centred = block.astype(jnp.float32) - mean
+            out_ref[k, :, part] = head - mean * gain
+            piece = start // stretch
+            line = pl.ds(cells + start % stretch, step)
+            out_ref[k, piece : piece + 1, line] = mean
+            out_ref[k, pieces + piece : pieces + piece + 1, line] = jnp.sum(
+                centred * centred, axis=0, keepdims=True
+            )
+        out_ref[k, :, cells + stretch :] = jnp.broadcast_to(gain, (heads, 128))
+
+
+def merge_sums(count, own_ref, other_ref, kept_ref, sent_ref):
+    heads, width = kept_ref.shape
+    pieces = heads // 2
+    stretch = (width - 128) // (pieces + 1)
+    cells = pieces * stretch
+    high = lax.axis_index("ch") // 2
+    step = 512
+    for slot, out_ref in ((high, kept_ref), (1 - high, sent_ref)):
+        gain_own = own_ref[slot, :, cells + stretch :]
+        gain_other = other_ref[slot, :, cells + stretch :]
+        half_gain = 0.5 * (gain_own - gain_other)[:, 0:1]
+        out_ref[:, cells + stretch :] = gain_own + gain_other
+        for start in range(cells, cells + stretch, step):
+            part = pl.ds(start, step)
+            own = own_ref[slot, :, part]
+            other = other_ref[slot, :, part]
+            apart = (own - other)[0:pieces]
+            both = own + other
+            out_ref[:, part] = jnp.concatenate(
+                [0.5 * both[0:pieces], both[pieces:] + apart * apart * (0.5 * count)], axis=0
+            )
+        for start in range(0, cells, step):
+            part = pl.ds(start, step)
+            piece = start // stretch
+            line = pl.ds(cells + start % stretch, step)
+            apart = (
+                own_ref[slot, piece : piece + 1, line] - other_ref[slot, piece : piece + 1, line]
+            )
+            out_ref[:, part] = own_ref[slot, :, part] + other_ref[slot, :, part] + apart * half_gain
+
+
+def pair_bias(extent, own_ref, far_ref, out_ref, lines):
+    heads, width = own_ref.shape
+    half = extent // 2
+    pieces = heads // 2
+    stretch = (width - 128) // (pieces + 1)
+    cells = pieces * stretch
+    gain = own_ref[:, cells + stretch :] - far_ref[:, cells + stretch :]
+    half_gain = 0.5 * gain[:, 0:1]
+    step = 512
+    for start in range(0, cells, step):
+        part = pl.ds(start, step)
+        piece = start // stretch
+        line = pl.ds(cells + start % stretch, step)
+        mean = slice(piece, piece + 1)
+        square = slice(pieces + piece, pieces + piece + 1)
+        apart = own_ref[mean, line] - far_ref[mean, line]
+        spread = own_ref[square, line] + far_ref[square, line] + apart * apart * (C_Z / 4.0)
+        inverse = lax.rsqrt(spread * (1.0 / C_Z) + EPS)
+        head = (own_ref[:, part] + far_ref[:, part] + apart * half_gain) * inverse
+        for inner in range(step // 128):
+            lines[pl.ds(start // 128 + inner, heads, stride=half), :] = head[
+                :, inner * 128 : (inner + 1) * 128
+            ]
+    out_ref[...] = lines[...].astype(jnp.bfloat16)
+
+
+def project(extent, rows, tiles, place_ref, *refs):
+    tile_refs, weight_refs = refs[:tiles], refs[tiles : tiles + 4]
+    gain_ref = refs[tiles + 4]
+    key_ref, value_ref, query_ref, gate_ref, chain_ref, stack = refs[tiles + 5 :]
+    lines = rows * extent
+    slots = chain_ref.shape[0]
+    for m in range(tiles):
+        stack[m] = tile_refs[m][...]
+    gain = gain_ref[...]
+    weights = [
+        jnp.concatenate([ref[kind] for ref in weight_refs], axis=0) for kind in range(4)
+    ]
+    for k in range(slots):
+        place = place_ref[k, 0]
+        tile = stack[place, 0:lines, :].astype(jnp.float32)
+        chain_ref[k] = stack[place, lines : lines + 8, 0:128].astype(jnp.float32)
+        normed = standardized(tile, gain).astype(jnp.bfloat16)
+        if k == 0:
+            put(query_ref, dot(normed, weights[0], BOTH_LAST).astype(jnp.bfloat16).astype(jnp.float32))
+            gate_ref[...] = dot(normed, weights[3], BOTH_LAST).astype(jnp.bfloat16)
+        keys = dot(normed, weights[1], BOTH_LAST).astype(jnp.bfloat16)
+        values = dot(normed, weights[2], BOTH_LAST).astype(jnp.bfloat16)
+        for s in range(rows):
+            part = slice(s * extent, (s + 1) * extent)
+            key_ref[s, k * extent : (k + 1) * extent, :] = keys[part]
+            value_ref[s, k * extent : (k + 1) * extent, :] = values[part]
+
+
+def attention(extent, rows, *refs):
+    key_ref, value_ref, query_ref, gate_ref, key_chain_ref, tile_ref = refs[:6]
+    weight_refs = refs[6:10]
+    bias_refs = refs[10:14]
+    chain_ref, chain_gain_ref, gain_ref, open_ref = refs[14:18]
+    row_ref, right_ref, pair, bias, attended = refs[18:]
+    slots = key_chain_ref.shape[0]
+    heads = FOCUS_NUMBER
+    local_heads = heads // 4
+    width = row_ref.shape[1]
+    half = extent // 2
+    lines = rows * extent
+    group = lax.axis_index("ch")
+    for m in range(4):
+        other = group ^ m
+        pair[2 * lax.rem(other, 2) + other // 2] = bias_refs[m][...]
+
+    low = lax.broadcasted_iota(jnp.int32, (half, 128), 1) < extent
+    for k in range(0, slots, 2):
+        chain = jnp.where(low[0:1], key_chain_ref[k, 0:1], key_chain_ref[k + 1, 0:1])
+        is_open = jnp.where(low, open_ref[k : k + 1, :], open_ref[k + 1 : k + 2, :]) > 0.0
+        same = [
+            (chain_ref[p * half : (p + 1) * half, :] == chain).astype(jnp.float32)
+            for p in range(2)
+        ]
+        lanes = slice((k // 2) * 128, (k // 2 + 1) * 128)
+        for h in range(heads):
+            rows_h = slice(h * half, (h + 1) * half)
+            zero = pair[k, rows_h, :].astype(jnp.float32)
+            one = pair[k + 1, rows_h, :].astype(jnp.float32)
+            joined = (
+                jnp.where(low, zero, pltpu.roll(one, extent, 1)),
+                jnp.where(low, pltpu.roll(zero, extent, 1), one),
+            )
+            for p in range(2):
+                value = joined[p] + chain_gain_ref[h : h + 1, :] * same[p]
+                bias[p, rows_h, lanes] = jnp.where(is_open, value, MASKED)
+
+    head_lane = lane_block((half, width), FOCUS_BREADTH)
+    for s in range(rows):
+        for p in range(2):
+            asked = take_every(query_ref, s * extent + p, half, 2)
+            asked = jnp.concatenate(
+                [jnp.where(head_lane == h, asked, 0.0) for h in range(heads)], axis=0
+            ).astype(jnp.bfloat16)
+            scores = dot(asked, key_ref[s], BOTH_LAST) * FOCUS_BREADTH ** (-0.5)
+            parts = []
+            for h in range(heads):
+                index = (group ^ (h // local_heads)) * local_heads + h % local_heads
+                start = pl.multiple_of(index * half, half)
+                parts.append(
+                    scores[h * half : (h + 1) * half] + bias[p, pl.ds(start, half), :]
+                )
+            scores = jnp.concatenate(parts, axis=0)
+            peak = jnp.max(scores, axis=1, keepdims=True)
+            exponent = jnp.exp(scores - peak)
+            share = 1.0 / jnp.sum(exponent, axis=1, keepdims=True)
+            weight = (exponent * share).astype(jnp.bfloat16)
+            mixed = dot(weight, value_ref[s], ACROSS)
+            kept = jnp.zeros((half, width), jnp.float32)
+            for h in range(heads):
+                kept = kept + jnp.where(head_lane == h, mixed[h * half : (h + 1) * half], 0.0)
+            put_every(attended, s * extent + p, 2, kept)
+    gates = gate_ref[...].astype(jnp.float32)
+    gated = (take(attended) * jax.nn.sigmoid(gates)).astype(jnp.bfloat16)
+    out_weight = jnp.concatenate([ref[4] for ref in weight_refs], axis=0)
+    change = dot(gated, out_weight, ACROSS)
+    updated = (tile_ref[0:lines, :].astype(jnp.float32) + change).astype(jnp.bfloat16)
+    row_ref[...] = updated
+    opm = standardized(updated.astype(jnp.float32), gain_ref[...]).astype(jnp.bfloat16)
+    factor = weight_refs[0][5].astype(jnp.float32)
+    for ref in weight_refs[1:]:
+        factor = factor + ref[5].astype(jnp.float32)
+    factor = factor[0:PRODUCT_FEATURE].astype(jnp.bfloat16)
+    right_ref[...] = dot(factor, opm, BOTH_LAST).astype(jnp.bfloat16)
+
+
+def product_tables(*refs):
+    piece_refs = refs[:4]
+    table_ref, stack, turned, lined = refs[4:]
+    features, narrow, channels = stack.shape[1:]
+    share = channels // 4
+    group = lax.axis_index("ch")
+    deep = piece_refs[0].shape[1]
+    for m in range(4):
+        for i in range(features * narrow // deep):
+            part = piece_refs[m][6 + i // 2, :, (i % 2) * 128 : (i % 2 + 1) * 128]
+            few = deep // narrow
+            stack[group ^ m, i * few : (i + 1) * few] = part.astype(
+                jnp.float32
+            ).reshape(few, narrow, channels)
+    own = pl.multiple_of(group * share, share)
+    lines = features // 4
+    for block in range(lines):
+        tall = jnp.concatenate(
+            [
+                stack[m, block * 4 + i]
+                for i in range(4)
+                for m in range(4)
+            ],
+            axis=0,
+        )
+        turned[...] = tall.T
+        lined[pl.ds(block, share, stride=lines), :] = turned[pl.ds(own, share), :]
+    lanes = lane_block((lines, 128), features)
+    for z in range(share):
+        rows = lined[z * lines : (z + 1) * lines, :]
+        moved = [rows] + [pltpu.roll(rows, by * features, 1) for by in range(1, 4)]
+        parts = [
+            jnp.where(lanes == s, moved[(s - i) % 4], 0.0) for s in range(4) for i in range(4)
+        ]
+        table_ref[z // 2, :, (z % 2) * 128 : (z % 2 + 1) * 128] = jnp.concatenate(
+            parts, axis=0
+        ).astype(jnp.bfloat16)
+
+
+def left_tables(extent, rows, *refs):
+    piece_refs = refs[:4]
+    factor_ref, gain_ref, weight_ref = refs[4:7]
+    table_ref, result_ref = refs[7:9]
+    spread, natural = refs[9:]
+    half = extent // 2
+    features = PRODUCT_FEATURE
+    lines = rows * extent
+    factor = jnp.concatenate([factor_ref[...]] * 4, axis=0)
+    lanes = lane_block((lines, 128), features)
+    left = jnp.zeros((lines, 128), jnp.float32)
+    for m in range(4):
+        piece = piece_refs[m][...]
+        group = lax.axis_index("ch") ^ m
+        for s in range(rows):
+            result_ref[group * rows + s] = piece[s * extent : (s + 1) * extent]
+        normed = standardized(piece.astype(jnp.float32), gain_ref[...]).astype(jnp.bfloat16)
+        left = left + jnp.where(lanes == m, dot(normed, factor, BOTH_LAST), 0.0)
+    natural[...] = left
+    left = jnp.concatenate(
+        [
+            natural[pl.ds(s * extent + p, half, stride=2), :]
+            for p in range(2)
+            for s in range(rows)
+        ],
+        axis=0,
+    ).astype(jnp.bfloat16)
+    pairs = weight_ref.shape[0]
+    for z in range(pairs):
+        table = dot(left, weight_ref[z], ACROSS)
+        for b in range(2 * rows):
+            for q in range(2):
+                spread[b, pl.ds(2 * z + q, half, stride=2 * pairs), :] = table[
+                    b * half : (b + 1) * half, q * 128 : (q + 1) * 128
+                ]
+    for b in range(2 * rows):
+        table_ref[:, b * 128 : (b + 1) * 128] = spread[b].astype(jnp.bfloat16)
+
+
+def pick(place_ref, even_ref, odd_ref, out_ref):
+    for k in range(out_ref.shape[0]):
+        place = place_ref[k, 0]
+        even = even_ref[place // 2]
+        odd = odd_ref[place // 2]
+        out_ref[k] = jnp.where(lax.rem(place, 2) == 0, even, odd)
+
+
+def pair_update(extent, rows, scale, open_ref, table_ref, pair_ref, offset_ref, *refs):
+    piece_refs = refs[:4]
+    out_ref, right, held, sems = refs[4:]
+    slots, channels, cells = pair_ref.shape
+    low = lax.broadcasted_iota(jnp.int32, (4 * piece_refs[0].shape[1], 128), 1) < extent
+    for k in range(slots):
+        one = jnp.concatenate([ref[k] for ref in piece_refs], axis=0).astype(jnp.float32)
+        turned = pltpu.roll(one, extent, 1)
+        depth = one.shape[0]
+        for p in range(2):
+            for s in range(rows):
+                value = one if s == p else turned
+                value = jnp.where(low if p == 0 else jnp.logical_not(low), value, 0.0)
+                start = (p * rows + s) * depth
+                right[start : start + depth, k * 128 : (k + 1) * 128] = value.astype(
+                    jnp.bfloat16
+                )
+    offset = offset_ref[...]
+    keep = [open_ref[k : k + 1, :] for k in range(slots)]
+    steps = sems.shape[0]
+    stretch = cells // steps
+    deep = stretch // 128
+    copies = []
+    for i in range(steps):
+        total = dot(
+            table_ref[i * deep * channels : (i + 1) * deep * channels, :], right[...], ACROSS
+        )
+        for k in range(slots):
+            for line in range(deep):
+                update = total[line * channels : (line + 1) * channels, k * 128 : (k + 1) * 128]
+                update = update * scale + offset
+                cell = slice((i * deep + line) * 128, (i * deep + line + 1) * 128)
+                held[k, :, cell] = (
+                    pair_ref[k, :, cell].astype(jnp.float32) + keep[k] * update
+                ).astype(jnp.bfloat16)
+        part = pl.ds(i * stretch, stretch)
+        copies.append(
+            pltpu.make_async_copy(held.at[:, :, part], out_ref.at[:, :, part], sems.at[i])
+        )
+        copies[-1].start()
+    for copy in copies:
+        copy.wait()
+
+
+def on_device_small(*arguments):
+    return small(*arguments)
+
+
+def small(
+    sequence_matrix,
+    couple_matrix,
+    block_target_entry,
+    block_present_flag,
+    amino_strand,
+    sequence_scaling_factor,
+    query_key_value_matrix,
+    focus_result_matrix,
+    strand_focus_offset,
+    couple_scaling_factor,
+    focus_offset_matrix,
+    product_scaling_factor,
+    first_factor_matrix,
+    second_factor_matrix,
+    product_result_matrix,
+    product_result_offset,
+):
+    groups = lax.axis_size("ch")
+    tiles = lax.axis_size("res")
+    sequences, extent, width = sequence_matrix.shape
+    slots, channels, cells = couple_matrix.shape
+    rows = sequences // groups
+    lines = rows * extent
+    heads = FOCUS_NUMBER
+    features = PRODUCT_FEATURE
+    half = extent // 2
+    inner = query_key_value_matrix.shape[2]
+    block = width // 128
+
+    def vmem(*shape):
+        return pltpu.VMEM(shape, jnp.float32)
+
+    def short(*shape):
+        return jax.ShapeDtypeStruct(shape, jnp.bfloat16)
+
+    def full(*shape):
+        return jax.ShapeDtypeStruct(shape, jnp.float32)
+
+    def in_hbm(values):
+        return pltpu.with_memory_space_constraint(values, pltpu.HBM)
+
+    second_rows = second_factor_matrix.T
+    first_rows = first_factor_matrix.T
+    product_rows = product_result_matrix.transpose(1, 2, 0).reshape(-1, C_Z)
+    (
+        tile_piece,
+        weight_piece,
+        pair_field,
+        sum_weights,
+        gain_one,
+        gain_two,
+        first_rows,
+        offset,
+        chain_column,
+        chain_gain,
+        place,
+        present,
+    ) = call(
+        functools.partial(prepare, extent, rows),
+        (
+            short(lines + 8, width),
+            short(6 + product_rows.size // (inner * width), inner, width),
+            short(slots, channels, cells),
+            short(4 * heads, channels),
+            full(1, width),
+            full(1, width),
+            short(features, width),
+            full(channels, 128),
+            full(extent, 128),
+            full(heads, 128),
+            jax.ShapeDtypeStruct((slots, 128), jnp.int32),
+            full(slots, 128),
+        ),
+        jax.tree.map(
+            in_hbm,
+            (
+            sequence_matrix,
+            couple_matrix,
+            query_key_value_matrix.transpose(0, 2, 1),
+            focus_result_matrix,
+            second_rows,
+            amino_strand.reshape(1, extent),
+            couple_scaling_factor.reshape(1, channels),
+            focus_offset_matrix.T,
+            sequence_scaling_factor.reshape(1, width),
+            product_scaling_factor.reshape(1, width),
+            first_rows,
+            product_result_offset.reshape(1, channels),
+            strand_focus_offset.reshape(1, heads),
+            product_rows,
+            block_target_entry,
+            block_present_flag,
+            ),
+        ),
+        [pl.BlockSpec(memory_space=pltpu.HBM)] * 16,
+        [
+            pltpu.VMEM(second_rows.shape, jnp.bfloat16),
+            pltpu.VMEM((1, extent), jnp.int32),
+            vmem(1, channels),
+            vmem(heads, channels),
+            pltpu.VMEM((features, width), jnp.bfloat16),
+            vmem(1, channels),
+            vmem(1, heads),
+            pltpu.SMEM((1, slots), jnp.int32),
+            pltpu.SMEM((1, slots), jnp.int32),
+            vmem(block, features, 128),
+            vmem(extent, 128),
+            pltpu.SemaphoreType.DMA((14 + rows + product_rows.shape[0] // inner,)),
+        ],
+        1_000_000,
+        3_000_000,
+    )
+
+    weight_pieces = over_groups(weight_piece, True)
+
+    tile_pieces = over_tiles(tile_piece)
+
+    sums_shape = (slots // 2, heads, cells + cells // (heads // 2) + 128)
+
+    def sums_of(keep):
+        return call(
+            functools.partial(pair_sums, keep),
+            jax.ShapeDtypeStruct(sums_shape, jnp.float32),
+            (sum_weights, pair_field),
+            [spec()] * 2,
+            [],
+            2 * slots // 2 * cells * channels * 4 * heads,
+            couple_matrix.size,
+        )
+
+    given = sums_of(False)
+    taken = flip(given, "ch", 1)
+    kept = sums_of(True)
+    merged, sent = call(
+        functools.partial(merge_sums, channels),
+        (full(*sums_shape[1:]), full(*sums_shape[1:])),
+        (kept, taken),
+        [spec()] * 2,
+        [],
+        given.size * 4,
+        given.size * 12,
+    )
+    far_sums = flip(sent, "ch", 2)
+    own_bias = call(
+        functools.partial(pair_bias, extent),
+        short(heads * half, 128),
+        (merged, far_sums),
+        [spec()] * 2,
+        [vmem(heads * half, 128)],
+        given.size * 4,
+        given.size * 8,
+    )
+    bias_pieces = over_groups(own_bias, True)
+
+    own_weights = call(
+        product_tables,
+        short(channels // 2, 128, 256),
+        tuple(weight_pieces),
+        [spec()] * 4,
+        [
+            vmem(groups, features, features // groups, C_Z),
+            vmem(C_Z, 128),
+            vmem(channels * features // 4, 128),
+        ],
+        1_000_000,
+        2_000_000,
+    )
+
+    keys, values, query, gates, key_chain = call(
+        functools.partial(project, extent, rows, tiles),
+        (
+            short(rows, slots * extent, width),
+            short(rows, slots * extent, width),
+            full(block, lines, 128),
+            short(lines, width),
+            full(slots, 8, 128),
+        ),
+        (place, *tile_pieces, *weight_pieces, gain_one),
+        [spec()] * (tiles + 6),
+        [pltpu.VMEM((tiles, lines + 8, width), jnp.bfloat16)],
+        200_000_000,
+        2_000_000,
+    )
+    row_piece, right_piece = call(
+        functools.partial(attention, extent, rows),
+        (short(lines, width), short(features, lines)),
+        (
+            keys,
+            values,
+            query,
+            gates,
+            key_chain,
+            tile_piece,
+            *weight_pieces,
+            *bias_pieces,
+            chain_column,
+            chain_gain,
+            gain_two,
+            present,
+        ),
+        [spec()] * 18,
+        [
+            pltpu.VMEM((slots, heads * half, 128), jnp.bfloat16),
+            vmem(2, heads * half, slots * extent),
+            vmem(block, lines, 128),
+        ],
+        600_000_000,
+        3_000_000,
+    )
+
+    right_pieces = [right_piece] + [flip(right_piece, "res", bits) for bits in range(2, tiles, 2)]
+    stacked = jnp.stack(right_pieces)
+    turned = flip(stacked, "res", 1)
+    picked = call(
+        pick,
+        short(slots, features, lines),
+        (place, stacked, turned),
+        [spec()] * 3,
+        [],
+        1000,
+        200_000,
+    )
+    right_tiles = over_groups(picked, False)
+    row_pieces = over_groups(row_piece, False)
+
+    table, sequence_result_matrix = call(
+        functools.partial(left_tables, extent, rows),
+        (
+            short(half * channels, 2 * rows * 128),
+            short(sequences, extent, width),
+        ),
+        (*row_pieces, first_rows, gain_two, own_weights),
+        [spec()] * 7,
+        [vmem(2 * rows, half * channels, 128), vmem(lines, 128)],
+        300_000_000,
+        3_000_000,
+    )
+
+    steps = 8
+    pairwise_output = pl.pallas_call(
+        functools.partial(pair_update, extent, rows, 1.0 / sequences),
+        out_shape=jax.ShapeDtypeStruct(couple_matrix.shape, jnp.bfloat16),
+        in_specs=[spec()] * 8,
+        out_specs=pl.BlockSpec(memory_space=pl.ANY),
+        scratch_shapes=[
+            pltpu.VMEM((table.shape[1], slots * 128), jnp.bfloat16),
+            pltpu.VMEM(couple_matrix.shape, jnp.bfloat16),
+            pltpu.SemaphoreType.DMA((steps,)),
+        ],
+        name="pair_update",
+        cost_estimate=pl.CostEstimate(
+            flops=600_000_000, bytes_accessed=3_000_000, transcendentals=0
+        ),
+        compiler_params=pltpu.CompilerParams(vmem_limit_bytes=VMEM_LIMIT),
+    )(present, table, pair_field, offset, *right_tiles)
+    return (sequence_result_matrix, pairwise_output)
+
+
 def solution(mesh):
+    few = mesh.shape["res"] <= 8 and mesh.shape["ch"] == 4
     return jax.shard_map(
-        on_device,
+        on_device_small if few else on_device,
         mesh=mesh,
         in_specs=(
             P(None, "res", None),

time: 452 us -> 55.8 us (0.12)
  local copies, waits for them, and re-layouts: 146 us -> 0 us
  blocking collectives: 127 us -> 0 us
  waiting for transfers between devices: 109 us -> 17.6 us
  other arithmetic: 21.8 us -> 0.01 us
  matrix products: 17.3 us -> 0 us
  starting transfers between devices: 13.2 us -> 28 us
  between operations: 15.5 us -> 0.78 us
  Pallas kernels: 0 us -> 9.31 us
    all_gather x4 -> x0, blocking collectives: 99.2 us -> none  [the longest x1 33.1 us: on_device(): shard_piece = lax.all_gather(right_projected, 'res', axis=1, tiled=True)]
    convert_element_type x12 -> x0, local copies, waits for them, and re-layouts: 91.3 us -> none  [the longest x8 90.9 us: outer_one(): product = product.reshape(block_extent, PRODUCT_FEATURE, block_extent, na...]
    reduce_scatter x1 -> x0, waiting for transfers between devices: 68.8 us -> none  [on_device(): summed = lax.psum_scatter(partials, 'ch', scatter_dimension=1, tiled=True)]
    psum x2 -> x0, waiting for transfers between devices: 31.8 us -> none  [the longest x1 31.8 us: on_device(): head_total = lax.psum(partial_out, 'ch')]
    unnamed x2 -> x0, blocking collectives: 28.2 us -> none
    ppermute x0 -> x25, starting transfers between devices: none -> 28 us  [flip(): return lax.ppermute(values, axis, [(i, i ^ bits) for i in range(size)])]
    reshape x12 -> x0, local copies, waits for them, and re-layouts: 24.2 us -> none  [the longest x4 22.7 us: outer_one(): product = product.reshape(block_extent, PRODUCT_FEATURE, block_extent, na...]
    ppermute x0 -> x25, waiting for transfers between devices: none -> 17.6 us  [flip(): return lax.ppermute(values, axis, [(i, i ^ bits) for i in range(size)])]
  transfers between devices with their start and end apart: 5 -> 25, of which waited for: 3 -> 9; matrix products, arithmetic and copies ran while one was open for 4% -> 0% of each run, Pallas kernels for 0% -> 7%
where the time goes in v1:
time: 55.8 us; the launch traced here: 55.6 us
  starting transfers between devices  28 us (50%)
  waiting for transfers between devices  17.6 us (32%)
  Pallas kernels  9.31 us (17%)
  between operations  0.78 us (1%)
    ppermute x25, starting transfers between devices, flip(): return lax.ppermute(values, axis, [(i, i ^ bits) for i in range(size)])  28 us
    ppermute x25, waiting for transfers between devices, flip(): return lax.ppermute(values, axis, [(i, i ^ bits) for i in range(size)])  17.6 us
    pallas_call x10, Pallas kernels, call(): pl.pallas_call(body, out_shape=out, in_specs=specs, out_specs=out_specs,...  7.66 us
    pallas_call x1, Pallas kernels, small(): pl.pallas_call(functools.partial(pair_update, extent, rows, 1.0 / sequenc...  1.65 us
  transfers between devices with their start and end apart: 25, of which 9 were waited for; matrix products, arithmetic and copies ran while one was open for 0% of the time, Pallas kernels for 7%

profile of v1, /device:TPU:0, one launch (start us, length us, event | category | flops | bytes accessed | tf_op | source)
XLA Modules:
  0.0 55.6 jit_solution(13111071910395582289)
XLA Ops:
  0.6 1.6 %shard_map.167 = (bf16[136,256]{1,0:T(8,128)(2,1)S(1)}, bf16[8,64,256]{2,1,0:T(8,128)(2,1)S(1)}, bf16[4,32,4096]{2,1,0:T(8,128)(2,1)S(1)}, bf16[32,32]{1,0:T(8,1...) custom-call(bf16[8,64,256]{2,1,0:T(8,128)(2,1)} %refs_0_.1, ...), custom_call_target="tpu_custom_call" | custom-call | flops 1000000 | bytes 3000000 | tf_op jit(solution)/shard_map/pallas_call | solution.py:292
  2.3 0.4 shard_map.170
  2.7 0.6 %collective-permute-start.10 = (f32[2,8,5248]{2,1,0:T(8,128)S(1)}, f32[2,8,5248]{2,1,0:T(8,128)S(1)}, u32[]{:S(2)}, u32[]{:S(2)}) collective-permute-start(f32[2,8,5248]{2,1,0:T(8,128)S(1)} %shard_map.170), channel_id=1, source_target_pairs={{0,1},{1,0},{2,3},{3,2},{4,5},{5,4},{6,7},{7,6},{8,9},{9,8},{10,11... | collective-permute-start | bytes 1007624 | tf_op jit(solution)/shard_map/ppermute | solution.py:226
  3.3 2.5 %collective-permute-start.8 = (bf16[8,64,256]{2,1,0:T(8,128)(2,1)S(1)}, bf16[8,64,256]{2,1,0:T(8,128)(2,1)S(1)}, u32[]{:S(2)}, u32[]{:S(2)}) collective-permute-start(bf16[8,64,256]{2,1,0:T(8,128)(2,1)S(1)} %get-tuple-element.27.refs_8_.refs_6_.refs_0_), channel_id=1, source_target_pairs={{0,2},{1,3},{2,0},{3,1},{4,6},{5,7},{6,4},{7,5},{8,10},{9,11},{10,... | collective-permute-start | bytes 786440 | tf_op jit(solution)/shard_map/ppermute | solution.py:226
  5.8 0.4 shard_map.169.own_ref
  6.2 0.1 shard_map.171
  6.4 1.2 %collective-permute-start.11 = (f32[8,5248]{1,0:T(8,128)S(1)}, f32[8,5248]{1,0:T(8,128)S(1)}, u32[]{:S(2)}, u32[]{:S(2)}) collective-permute-start(f32[8,5248]{1,0:T(8,128)S(1)} %get-tuple-element.37), channel_id=1, source_target_pairs={{0,2},{1,3},{2,0},{3,1},{4,6},{5,7},{6,4},{7,5},{8,10},{9,11},{10,... | collective-permute-start | bytes 503816 | tf_op jit(solution)/shard_map/ppermute | solution.py:226
  7.5 1.6 %collective-permute-start.1 = (bf16[136,256]{1,0:T(8,128)(2,1)S(1)}, bf16[136,256]{1,0:T(8,128)(2,1)S(1)}, u32[]{:S(2)}, u32[]{:S(2)}) collective-permute-start(bf16[136,256]{1,0:T(8,128)(2,1)S(1)} %get-tuple-element.26.refs_0_.refs_5_), channel_id=1, source_target_pairs={{0,8},{4,12},{8,0},{12,4},{16,24},{20,28},{24,16},{28,20},{1,9},{5... | collective-permute-start | bytes 208904 | tf_op jit(solution)/shard_map/ppermute | solution.py:226
  9.1 0.0 collective-permute-start.7
  9.1 3.8 %collective-permute-done.8.refs_10_.refs_8_.refs_2_ = bf16[8,64,256]{2,1,0:T(8,128)(2,1)S(1)} collective-permute-done((bf16[8,64,256]{2,1,0:T(8,128)(2,1)S(1)}, bf16[8,64,256]{2,1,0:T(8,128)(2,1)S(1)}, u32[]{:S(2)}, u32[]{:S(2)}) %collective-permute-start.8) | collective-permute-done | bytes 262176 | tf_op jit(solution)/shard_map/ppermute | solution.py:226
  13.0 0.0 collective-permute-start.9
  13.0 3.1 %collective-permute-start.3 = (bf16[136,256]{1,0:T(8,128)(2,1)S(1)}, bf16[136,256]{1,0:T(8,128)(2,1)S(1)}, u32[]{:S(2)}, u32[]{:S(2)}) collective-permute-start(bf16[136,256]{1,0:T(8,128)(2,1)S(1)} %get-tuple-element.26.refs_0_.refs_5_), channel_id=1, source_target_pairs={{0,16},{4,20},{8,24},{12,28},{16,0},{20,4},{24,8},{28,12},{1,17},{... | collective-permute-start | bytes 208904 | tf_op jit(solution)/shard_map/ppermute | solution.py:226
  16.1 0.0 collective-permute-done.1.refs_2_
  16.1 1.4 %collective-permute-start.5 = (bf16[136,256]{1,0:T(8,128)(2,1)S(1)}, bf16[136,256]{1,0:T(8,128)(2,1)S(1)}, u32[]{:S(2)}, u32[]{:S(2)}) collective-permute-start(bf16[136,256]{1,0:T(8,128)(2,1)S(1)} %get-tuple-element.26.refs_0_.refs_5_), channel_id=1, source_target_pairs={{0,24},{4,28},{8,16},{12,20},{16,8},{20,12},{24,0},{28,4},{1,25},{... | collective-permute-start | bytes 208904 | tf_op jit(solution)/shard_map/ppermute | solution.py:226
  17.5 3.2 %collective-permute-done.3.refs_4_ = bf16[136,256]{1,0:T(8,128)(2,1)S(1)} collective-permute-done((bf16[136,256]{1,0:T(8,128)(2,1)S(1)}, bf16[136,256]{1,0:T(8,128)(2,1)S(1)}, u32[]{:S(2)}, u32[]{:S(2)}) %collective-permute-start.3) | collective-permute-done | bytes 69664 | tf_op jit(solution)/shard_map/ppermute | solution.py:226
  20.6 3.3 %collective-permute-start = (bf16[136,256]{1,0:T(8,128)(2,1)S(1)}, bf16[136,256]{1,0:T(8,128)(2,1)S(1)}, u32[]{:S(2)}, u32[]{:S(2)}) collective-permute-start(bf16[136,256]{1,0:T(8,128)(2,1)S(1)} %get-tuple-element.26.refs_0_.refs_5_), channel_id=1, source_target_pairs={{0,4},{4,0},{8,12},{12,8},{16,20},{20,16},{24,28},{28,24},{1,5},{5... | collective-permute-start | bytes 208904 | tf_op jit(solution)/shard_map/ppermute | solution.py:226
  23.9 0.0 collective-permute-done.5.refs_6_
  23.9 0.0 collective-permute-start.2
  23.9 2.0 %collective-permute-start.4 = (bf16[136,256]{1,0:T(8,128)(2,1)S(1)}, bf16[136,256]{1,0:T(8,128)(2,1)S(1)}, u32[]{:S(2)}, u32[]{:S(2)}) collective-permute-start(bf16[136,256]{1,0:T(8,128)(2,1)S(1)} %collective-permute-done.3.refs_4_), channel_id=1, source_target_pairs={{0,4},{4,0},{8,12},{12,8},{16,20},{20,16},{24,28},{28,24},{1,5},{5... | collective-permute-start | bytes 208904 | tf_op jit(solution)/shard_map/ppermute | solution.py:226
  25.9 0.2 shard_map.172.refs_10_
  26.1 0.6 %collective-permute-done.refs_1_ = bf16[136,256]{1,0:T(8,128)(2,1)S(1)} collective-permute-done((bf16[136,256]{1,0:T(8,128)(2,1)S(1)}, bf16[136,256]{1,0:T(8,128)(2,1)S(1)}, u32[]{:S(2)}, u32[]{:S(2)}) %collective-permute-start) | collective-permute-done | bytes 69664 | tf_op jit(solution)/shard_map/ppermute | solution.py:226
  26.7 1.5 %collective-permute-start.13 = (bf16[256,128]{1,0:T(8,128)(2,1)S(1)}, bf16[256,128]{1,0:T(8,128)(2,1)S(1)}, u32[]{:S(2)}, u32[]{:S(2)}) collective-permute-start(bf16[256,128]{1,0:T(8,128)(2,1)S(1)} %shard_map.172.refs_10_), channel_id=1, source_target_pairs={{0,2},{1,3},{2,0},{3,1},{4,6},{5,7},{6,4},{7,5},{8,10},{9,11},{10,... | collective-permute-start | bytes 196616 | tf_op jit(solution)/shard_map/ppermute | solution.py:226
  28.2 0.4 collective-permute-done.2.refs_3_
  28.6 1.0 %collective-permute-start.6 = (bf16[136,256]{1,0:T(8,128)(2,1)S(1)}, bf16[136,256]{1,0:T(8,128)(2,1)S(1)}, u32[]{:S(2)}, u32[]{:S(2)}) collective-permute-start(bf16[136,256]{1,0:T(8,128)(2,1)S(1)} %collective-permute-done.5.refs_6_), channel_id=1, source_target_pairs={{0,4},{4,0},{8,12},{12,8},{16,20},{20,16},{24,28},{28,24},{1,5},{5... | collective-permute-start | bytes 208904 | tf_op jit(solution)/shard_map/ppermute | solution.py:226
  29.7 0.0 collective-permute-done.4.refs_5_
  29.7 0.0 collective-permute-start.12
  29.7 1.3 %collective-permute-done.13.refs_12_ = bf16[256,128]{1,0:T(8,128)(2,1)S(1)} collective-permute-done((bf16[256,128]{1,0:T(8,128)(2,1)S(1)}, bf16[256,128]{1,0:T(8,128)(2,1)S(1)}, u32[]{:S(2)}, u32[]{:S(2)}) %collective-permute-start.13) | collective-permute-done | bytes 65568 | tf_op jit(solution)/shard_map/ppermute | solution.py:226
  31.0 0.0 collective-permute-start.14
  31.0 1.9 %collective-permute-done.6.refs_7_ = bf16[136,256]{1,0:T(8,128)(2,1)S(1)} collective-permute-done((bf16[136,256]{1,0:T(8,128)(2,1)S(1)}, bf16[136,256]{1,0:T(8,128)(2,1)S(1)}, u32[]{:S(2)}, u32[]{:S(2)}) %collective-permute-start.6) | collective-permute-done | bytes 69664 | tf_op jit(solution)/shard_map/ppermute | solution.py:226
  33.0 0.8 %shard_map.168 = (bf16[2,256,256]{2,1,0:T(8,128)(2,1)S(1)}, bf16[2,256,256]{2,1,0:T(8,128)(2,1)S(1)}, f32[2,128,128]{2,1,0:T(8,128)S(1)}, bf16[128,256]{1,0:T(8,128)(2,1)S(1)}, f32[4,8,128]{2,1,0:T(8,128)S(1)}) custom-call(s32[4,128]{1,0:T(4,128)S(1)} %get-tuple-element.25.place_ref, bf16[136,256]{1,0:T(8,128)(2,1)S(1)} %get-tuple-element.26.refs_0_.refs_5_, ...), custom_call_target="tpu_custom_call" | custom-call | flops 200000000 | bytes 2000000 | tf_op jit(solution)/shard_map/pallas_call | solution.py:292
  33.8 0.0 collective-permute-done.14.refs_13_
  33.8 1.7 %shard_map.173 = (bf16[128,256]{1,0:T(8,128)(2,1)S(1)}, bf16[32,128]{1,0:T(8,128)(2,1)S(1)}) custom-call(bf16[2,256,256]{2,1,0:T(8,128)(2,1)S(1)} %get-tuple-element.29.refs_0_, bf16[2,256,256]{2,1,0:T(8,128)(2,1)S(1)} %get-tuple-element.30.refs_1_, f32[2,128,128]{2,1,0:T(8,128)S(1)} %get-tuple-element.31.refs_2_, ...), custom_call_target="tpu_custom_call" | custom-call | flops 600000000 | bytes 3000000 | tf_op jit(solution)/shard_map/pallas_call | solution.py:292
  35.5 0.4 collective-permute-start.18
  35.8 3.6 %collective-permute-start.19 = (bf16[32,128]{1,0:T(8,128)(2,1)S(1)}, bf16[32,128]{1,0:T(8,128)(2,1)S(1)}, u32[]{:S(2)}, u32[]{:S(2)}) collective-permute-start(bf16[32,128]{1,0:T(8,128)(2,1)S(1)} %get-tuple-element.47), channel_id=1, source_target_pairs={{0,16},{4,20},{8,24},{12,28},{16,0},{20,4},{24,8},{28,12},{1,17},{... | collective-permute-start | bytes 24584 | tf_op jit(solution)/shard_map/ppermute | solution.py:226
  39.5 0.4 collective-permute-start.20
  39.9 1.5 %collective-permute-start.16 = (bf16[128,256]{1,0:T(8,128)(2,1)S(1)}, bf16[128,256]{1,0:T(8,128)(2,1)S(1)}, u32[]{:S(2)}, u32[]{:S(2)}) collective-permute-start(bf16[128,256]{1,0:T(8,128)(2,1)S(1)} %get-tuple-element.42.refs_0_), channel_id=1, source_target_pairs={{0,2},{1,3},{2,0},{3,1},{4,6},{5,7},{6,4},{7,5},{8,10},{9,11},{10,... | collective-permute-start | bytes 196616 | tf_op jit(solution)/shard_map/ppermute | solution.py:226
  41.4 0.4 collective-permute-start.17
  41.7 3.2 %collective-permute-done.20 = bf16[32,128]{1,0:T(8,128)(2,1)S(1)} collective-permute-done((bf16[32,128]{1,0:T(8,128)(2,1)S(1)}, bf16[32,128]{1,0:T(8,128)(2,1)S(1)}, u32[]{:S(2)}, u32[]{:S(2)}) %collective-permute-start.20) | collective-permute-done | bytes 8224 | tf_op jit(solution)/shard_map/ppermute | solution.py:226
  44.9 1.6 %collective-permute-start.21 = (bf16[4,32,128]{2,1,0:T(8,128)(2,1)S(1)}, bf16[4,32,128]{2,1,0:T(8,128)(2,1)S(1)}, u32[]{:S(2)}, u32[]{:S(2)}) collective-permute-start(bf16[4,32,128]{2,1,0:T(8,128)(2,1)S(1)} %pad_maximum_fusion.even_ref), channel_id=1, source_target_pairs={{0,4},{4,0},{8,12},{12,8},{16,20},{20,16},{24,28},{28,24},{1,5},{5... | collective-permute-start | bytes 98312 | tf_op jit(solution)/shard_map/ppermute | solution.py:226
  46.5 2.4 %collective-permute-done.21.odd_ref = bf16[4,32,128]{2,1,0:T(8,128)(2,1)S(1)} collective-permute-done((bf16[4,32,128]{2,1,0:T(8,128)(2,1)S(1)}, bf16[4,32,128]{2,1,0:T(8,128)(2,1)S(1)}, u32[]{:S(2)}, u32[]{:S(2)}) %collective-permute-start.21) | collective-permute-done | bytes 32800 | tf_op jit(solution)/shard_map/ppermute | solution.py:226
  48.9 0.1 shard_map.176.refs_0_
  49.0 0.1 collective-permute-start.22
  49.0 1.6 %collective-permute-start.23 = (bf16[4,32,128]{2,1,0:T(8,128)(2,1)S(1)}, bf16[4,32,128]{2,1,0:T(8,128)(2,1)S(1)}, u32[]{:S(2)}, u32[]{:S(2)}) collective-permute-start(bf16[4,32,128]{2,1,0:T(8,128)(2,1)S(1)} %shard_map.176.refs_0_), channel_id=1, source_target_pairs={{0,2},{1,3},{2,0},{3,1},{4,6},{5,7},{6,4},{7,5},{8,10},{9,11},{10,... | collective-permute-start | bytes 98312 | tf_op jit(solution)/shard_map/ppermute | solution.py:226
  50.6 0.3 collective-permute-start.24
  50.9 0.4 shard_map.174.refs_6_
  51.4 1.9 %shard_map.175 = (bf16[1024,512]{1,0:T(8,128)(2,1)S(1)}, bf16[8,64,256]{2,1,0:T(8,128)(2,1)}) custom-call(bf16[128,256]{1,0:T(8,128)(2,1)S(1)} %get-tuple-element.42.refs_0_, bf16[128,256]{1,0:T(8,128)(2,1)S(1)} %collective-permute-done.15.refs_1_, bf16[128,256]{1,0:T(8,128)(2,1)S(1)} %collective-permute-done.16.refs_2_, ...), custom_call_target="tpu_custom_call" | custom-call | flops 300000000 | bytes 3000000 | tf_op jit(solution)/shard_map/pallas_call | solution.py:292
  53.3 0.6 %collective-permute-done.24.refs_3_ = bf16[4,32,128]{2,1,0:T(8,128)(2,1)S(1)} collective-permute-done((bf16[4,32,128]{2,1,0:T(8,128)(2,1)S(1)}, bf16[4,32,128]{2,1,0:T(8,128)(2,1)S(1)}, u32[]{:S(2)}, u32[]{:S(2)}) %collective-permute-start.24) | collective-permute-done | bytes 32800 | tf_op jit(solution)/shard_map/ppermute | solution.py:226
  54.0 1.6 %pair_update.1 = bf16[4,32,4096]{2,1,0:T(8,128)(2,1)} custom-call(f32[4,128]{1,0:T(4,128)S(1)} %get-tuple-element.41.refs_17_.open_ref, bf16[1024,512]{1,0:T(8,128)(2,1)S(1)} %get-tuple-element.45.table_ref, bf16[4,32,4096]{2,1,0:T(8,128)(2,1)S(1)} %get-tuple-element.35.pair_ref, f32[32,128]{1,0:T(8,128)S(1)} %get-tuple-element.46.offset_ref, ...), custom_call_target="tpu_custom_call" | custom-call | flops 600000000 | bytes 3000000 | tf_op jit(solution)/shard_map/pair_update/pallas_call | solution.py:956
  (14 shorter events, 0.0 us)
Async XLA Ops:
  2.7 3.5 %collective-permute-start.10 = (f32[2,8,5248]{2,1,0:T(8,128)S(1)}, f32[2,8,5248]{2,1,0:T(8,128)S(1)}, u32[]{:S(2)}, u32[]{:S(2)}) collective-permute-start(f32[2,8,5248]{2,1,0:T(8,128)S(1)} %shard_map.170), channel_id=1, source_target_pairs={{0,1},{1,0},{2,3},{3,2},{4,5},{5,4},{6,7},{7,6},{8,9},{9,8},{10,11... | collective-permute-start | bytes 1007624 | tf_op jit(solution)/shard_map/ppermute | solution.py:226
  3.3 9.7 %collective-permute-start.8 = (bf16[8,64,256]{2,1,0:T(8,128)(2,1)S(1)}, bf16[8,64,256]{2,1,0:T(8,128)(2,1)S(1)}, u32[]{:S(2)}, u32[]{:S(2)}) collective-permute-start(bf16[8,64,256]{2,1,0:T(8,128)(2,1)S(1)} %get-tuple-element.27.refs_8_.refs_6_.refs_0_), channel_id=1, source_target_pairs={{0,2},{1,3},{2,0},{3,1},{4,6},{5,7},{6,4},{7,5},{8,10},{9,11},{10,... | collective-permute-start | bytes 786440 | tf_op jit(solution)/shard_map/ppermute | solution.py:226
  6.4 17.5 %collective-permute-start.11 = (f32[8,5248]{1,0:T(8,128)S(1)}, f32[8,5248]{1,0:T(8,128)S(1)}, u32[]{:S(2)}, u32[]{:S(2)}) collective-permute-start(f32[8,5248]{1,0:T(8,128)S(1)} %get-tuple-element.37), channel_id=1, source_target_pairs={{0,2},{1,3},{2,0},{3,1},{4,6},{5,7},{6,4},{7,5},{8,10},{9,11},{10,... | collective-permute-start | bytes 503816 | tf_op jit(solution)/shard_map/ppermute | solution.py:226
  7.5 8.6 %collective-permute-start.1 = (bf16[136,256]{1,0:T(8,128)(2,1)S(1)}, bf16[136,256]{1,0:T(8,128)(2,1)S(1)}, u32[]{:S(2)}, u32[]{:S(2)}) collective-permute-start(bf16[136,256]{1,0:T(8,128)(2,1)S(1)} %get-tuple-element.26.refs_0_.refs_5_), channel_id=1, source_target_pairs={{0,8},{4,12},{8,0},{12,4},{16,24},{20,28},{24,16},{28,20},{1,9},{5... | collective-permute-start | bytes 208904 | tf_op jit(solution)/shard_map/ppermute | solution.py:226
  9.1 23.8 %collective-permute-start.7 = (bf16[8,64,256]{2,1,0:T(8,128)(2,1)S(1)}, bf16[8,64,256]{2,1,0:T(8,128)(2,1)S(1)}, u32[]{:S(2)}, u32[]{:S(2)}) collective-permute-start(bf16[8,64,256]{2,1,0:T(8,128)(2,1)S(1)} %get-tuple-element.27.refs_8_.refs_6_.refs_0_), channel_id=1, source_target_pairs={{0,1},{1,0},{2,3},{3,2},{4,5},{5,4},{6,7},{7,6},{8,9},{9,8},{10,11... | collective-permute-start | bytes 786440 | tf_op jit(solution)/shard_map/ppermute | solution.py:226
  13.0 20.0 %collective-permute-start.9 = (bf16[8,64,256]{2,1,0:T(8,128)(2,1)S(1)}, bf16[8,64,256]{2,1,0:T(8,128)(2,1)S(1)}, u32[]{:S(2)}, u32[]{:S(2)}) collective-permute-start(bf16[8,64,256]{2,1,0:T(8,128)(2,1)S(1)} %collective-permute-done.8.refs_10_.refs_8_.refs_2_), channel_id=1, source_target_pairs={{0,1},{1,0},{2,3},{3,2},{4,5},{5,4},{6,7},{7,6},{8,9},{9,8},{10,11... | collective-permute-start | bytes 786440 | tf_op jit(solution)/shard_map/ppermute | solution.py:226
  13.0 7.6 %collective-permute-start.3 = (bf16[136,256]{1,0:T(8,128)(2,1)S(1)}, bf16[136,256]{1,0:T(8,128)(2,1)S(1)}, u32[]{:S(2)}, u32[]{:S(2)}) collective-permute-start(bf16[136,256]{1,0:T(8,128)(2,1)S(1)} %get-tuple-element.26.refs_0_.refs_5_), channel_id=1, source_target_pairs={{0,16},{4,20},{8,24},{12,28},{16,0},{20,4},{24,8},{28,12},{1,17},{... | collective-permute-start | bytes 208904 | tf_op jit(solution)/shard_map/ppermute | solution.py:226
  16.1 7.8 %collective-permute-start.5 = (bf16[136,256]{1,0:T(8,128)(2,1)S(1)}, bf16[136,256]{1,0:T(8,128)(2,1)S(1)}, u32[]{:S(2)}, u32[]{:S(2)}) collective-permute-start(bf16[136,256]{1,0:T(8,128)(2,1)S(1)} %get-tuple-element.26.refs_0_.refs_5_), channel_id=1, source_target_pairs={{0,24},{4,28},{8,16},{12,20},{16,8},{20,12},{24,0},{28,4},{1,25},{... | collective-permute-start | bytes 208904 | tf_op jit(solution)/shard_map/ppermute | solution.py:226
  20.6 6.1 %collective-permute-start = (bf16[136,256]{1,0:T(8,128)(2,1)S(1)}, bf16[136,256]{1,0:T(8,128)(2,1)S(1)}, u32[]{:S(2)}, u32[]{:S(2)}) collective-permute-start(bf16[136,256]{1,0:T(8,128)(2,1)S(1)} %get-tuple-element.26.refs_0_.refs_5_), channel_id=1, source_target_pairs={{0,4},{4,0},{8,12},{12,8},{16,20},{20,16},{24,28},{28,24},{1,5},{5... | collective-permute-start | bytes 208904 | tf_op jit(solution)/shard_map/ppermute | solution.py:226
  23.9 4.8 %collective-permute-start.2 = (bf16[136,256]{1,0:T(8,128)(2,1)S(1)}, bf16[136,256]{1,0:T(8,128)(2,1)S(1)}, u32[]{:S(2)}, u32[]{:S(2)}) collective-permute-start(bf16[136,256]{1,0:T(8,128)(2,1)S(1)} %collective-permute-done.1.refs_2_), channel_id=1, source_target_pairs={{0,4},{4,0},{8,12},{12,8},{16,20},{20,16},{24,28},{28,24},{1,5},{5... | collective-permute-start | bytes 208904 | tf_op jit(solution)/shard_map/ppermute | solution.py:226
  23.9 5.8 %collective-permute-start.4 = (bf16[136,256]{1,0:T(8,128)(2,1)S(1)}, bf16[136,256]{1,0:T(8,128)(2,1)S(1)}, u32[]{:S(2)}, u32[]{:S(2)}) collective-permute-start(bf16[136,256]{1,0:T(8,128)(2,1)S(1)} %collective-permute-done.3.refs_4_), channel_id=1, source_target_pairs={{0,4},{4,0},{8,12},{12,8},{16,20},{20,16},{24,28},{28,24},{1,5},{5... | collective-permute-start | bytes 208904 | tf_op jit(solution)/shard_map/ppermute | solution.py:226
  26.7 4.3 %collective-permute-start.13 = (bf16[256,128]{1,0:T(8,128)(2,1)S(1)}, bf16[256,128]{1,0:T(8,128)(2,1)S(1)}, u32[]{:S(2)}, u32[]{:S(2)}) collective-permute-start(bf16[256,128]{1,0:T(8,128)(2,1)S(1)} %shard_map.172.refs_10_), channel_id=1, source_target_pairs={{0,2},{1,3},{2,0},{3,1},{4,6},{5,7},{6,4},{7,5},{8,10},{9,11},{10,... | collective-permute-start | bytes 196616 | tf_op jit(solution)/shard_map/ppermute | solution.py:226
  28.6 4.3 %collective-permute-start.6 = (bf16[136,256]{1,0:T(8,128)(2,1)S(1)}, bf16[136,256]{1,0:T(8,128)(2,1)S(1)}, u32[]{:S(2)}, u32[]{:S(2)}) collective-permute-start(bf16[136,256]{1,0:T(8,128)(2,1)S(1)} %collective-permute-done.5.refs_6_), channel_id=1, source_target_pairs={{0,4},{4,0},{8,12},{12,8},{16,20},{20,16},{24,28},{28,24},{1,5},{5... | collective-permute-start | bytes 208904 | tf_op jit(solution)/shard_map/ppermute | solution.py:226
  29.7 4.1 %collective-permute-start.12 = (bf16[256,128]{1,0:T(8,128)(2,1)S(1)}, bf16[256,128]{1,0:T(8,128)(2,1)S(1)}, u32[]{:S(2)}, u32[]{:S(2)}) collective-permute-start(bf16[256,128]{1,0:T(8,128)(2,1)S(1)} %shard_map.172.refs_10_), channel_id=1, source_target_pairs={{0,1},{1,0},{2,3},{3,2},{4,5},{5,4},{6,7},{7,6},{8,9},{9,8},{10,11... | collective-permute-start | bytes 196616 | tf_op jit(solution)/shard_map/ppermute | solution.py:226
  31.0 2.8 %collective-permute-start.14 = (bf16[256,128]{1,0:T(8,128)(2,1)S(1)}, bf16[256,128]{1,0:T(8,128)(2,1)S(1)}, u32[]{:S(2)}, u32[]{:S(2)}) collective-permute-start(bf16[256,128]{1,0:T(8,128)(2,1)S(1)} %collective-permute-done.13.refs_12_), channel_id=1, source_target_pairs={{0,1},{1,0},{2,3},{3,2},{4,5},{5,4},{6,7},{7,6},{8,9},{9,8},{10,11... | collective-permute-start | bytes 196616 | tf_op jit(solution)/shard_map/ppermute | solution.py:226
  35.5 5.9 %collective-permute-start.18 = (bf16[32,128]{1,0:T(8,128)(2,1)S(1)}, bf16[32,128]{1,0:T(8,128)(2,1)S(1)}, u32[]{:S(2)}, u32[]{:S(2)}) collective-permute-start(bf16[32,128]{1,0:T(8,128)(2,1)S(1)} %get-tuple-element.47), channel_id=1, source_target_pairs={{0,8},{4,12},{8,0},{12,4},{16,24},{20,28},{24,16},{28,20},{1,9},{5... | collective-permute-start | bytes 24584 | tf_op jit(solution)/shard_map/ppermute | solution.py:226
  35.8 5.9 %collective-permute-start.19 = (bf16[32,128]{1,0:T(8,128)(2,1)S(1)}, bf16[32,128]{1,0:T(8,128)(2,1)S(1)}, u32[]{:S(2)}, u32[]{:S(2)}) collective-permute-start(bf16[32,128]{1,0:T(8,128)(2,1)S(1)} %get-tuple-element.47), channel_id=1, source_target_pairs={{0,16},{4,20},{8,24},{12,28},{16,0},{20,4},{24,8},{28,12},{1,17},{... | collective-permute-start | bytes 24584 | tf_op jit(solution)/shard_map/ppermute | solution.py:226
  39.5 5.4 %collective-permute-start.20 = (bf16[32,128]{1,0:T(8,128)(2,1)S(1)}, bf16[32,128]{1,0:T(8,128)(2,1)S(1)}, u32[]{:S(2)}, u32[]{:S(2)}) collective-permute-start(bf16[32,128]{1,0:T(8,128)(2,1)S(1)} %get-tuple-element.47), channel_id=1, source_target_pairs={{0,24},{4,28},{8,16},{12,20},{16,8},{20,12},{24,0},{28,4},{1,25},{... | collective-permute-start | bytes 24584 | tf_op jit(solution)/shard_map/ppermute | solution.py:226
  39.9 10.8 %collective-permute-start.15 = (bf16[128,256]{1,0:T(8,128)(2,1)S(1)}, bf16[128,256]{1,0:T(8,128)(2,1)S(1)}, u32[]{:S(2)}, u32[]{:S(2)}) collective-permute-start(bf16[128,256]{1,0:T(8,128)(2,1)S(1)} %get-tuple-element.42.refs_0_), channel_id=1, source_target_pairs={{0,1},{1,0},{2,3},{3,2},{4,5},{5,4},{6,7},{7,6},{8,9},{9,8},{10,11... | collective-permute-start | bytes 196616 | tf_op jit(solution)/shard_map/ppermute | solution.py:226
  39.9 11.5 %collective-permute-start.16 = (bf16[128,256]{1,0:T(8,128)(2,1)S(1)}, bf16[128,256]{1,0:T(8,128)(2,1)S(1)}, u32[]{:S(2)}, u32[]{:S(2)}) collective-permute-start(bf16[128,256]{1,0:T(8,128)(2,1)S(1)} %get-tuple-element.42.refs_0_), channel_id=1, source_target_pairs={{0,2},{1,3},{2,0},{3,1},{4,6},{5,7},{6,4},{7,5},{8,10},{9,11},{10,... | collective-permute-start | bytes 196616 | tf_op jit(solution)/shard_map/ppermute | solution.py:226
  41.4 10.0 %collective-permute-start.17 = (bf16[128,256]{1,0:T(8,128)(2,1)S(1)}, bf16[128,256]{1,0:T(8,128)(2,1)S(1)}, u32[]{:S(2)}, u32[]{:S(2)}) collective-permute-start(bf16[128,256]{1,0:T(8,128)(2,1)S(1)} %get-tuple-element.42.refs_0_), channel_id=1, source_target_pairs={{0,3},{1,2},{2,1},{3,0},{4,7},{5,6},{6,5},{7,4},{8,11},{9,10},{10,... | collective-permute-start | bytes 196616 | tf_op jit(solution)/shard_map/ppermute | solution.py:226
  44.9 4.0 %collective-permute-start.21 = (bf16[4,32,128]{2,1,0:T(8,128)(2,1)S(1)}, bf16[4,32,128]{2,1,0:T(8,128)(2,1)S(1)}, u32[]{:S(2)}, u32[]{:S(2)}) collective-permute-start(bf16[4,32,128]{2,1,0:T(8,128)(2,1)S(1)} %pad_maximum_fusion.even_ref), channel_id=1, source_target_pairs={{0,4},{4,0},{8,12},{12,8},{16,20},{20,16},{24,28},{28,24},{1,5},{5... | collective-permute-start | bytes 98312 | tf_op jit(solution)/shard_map/ppermute | solution.py:226
  49.0 4.3 %collective-permute-start.22 = (bf16[4,32,128]{2,1,0:T(8,128)(2,1)S(1)}, bf16[4,32,128]{2,1,0:T(8,128)(2,1)S(1)}, u32[]{:S(2)}, u32[]{:S(2)}) collective-permute-start(bf16[4,32,128]{2,1,0:T(8,128)(2,1)S(1)} %shard_map.176.refs_0_), channel_id=1, source_target_pairs={{0,1},{1,0},{2,3},{3,2},{4,5},{5,4},{6,7},{7,6},{8,9},{9,8},{10,11... | collective-permute-start | bytes 98312 | tf_op jit(solution)/shard_map/ppermute | solution.py:226
  49.0 4.3 %collective-permute-start.23 = (bf16[4,32,128]{2,1,0:T(8,128)(2,1)S(1)}, bf16[4,32,128]{2,1,0:T(8,128)(2,1)S(1)}, u32[]{:S(2)}, u32[]{:S(2)}) collective-permute-start(bf16[4,32,128]{2,1,0:T(8,128)(2,1)S(1)} %shard_map.176.refs_0_), channel_id=1, source_target_pairs={{0,2},{1,3},{2,0},{3,1},{4,6},{5,7},{6,4},{7,5},{8,10},{9,11},{10,... | collective-permute-start | bytes 98312 | tf_op jit(solution)/shard_map/ppermute | solution.py:226
  50.6 3.4 %collective-permute-start.24 = (bf16[4,32,128]{2,1,0:T(8,128)(2,1)S(1)}, bf16[4,32,128]{2,1,0:T(8,128)(2,1)S(1)}, u32[]{:S(2)}, u32[]{:S(2)}) collective-permute-start(bf16[4,32,128]{2,1,0:T(8,128)(2,1)S(1)} %shard_map.176.refs_0_), channel_id=1, source_target_pairs={{0,3},{1,2},{2,1},{3,0},{4,7},{5,6},{6,5},{7,4},{8,11},{9,10},{10,... | collective-permute-start | bytes 98312 | tf_op jit(solution)/shard_map/ppermute | solution.py:226

commit v2 on v1

--- a/solution.py
+++ b/solution.py
@@ -476,39 +476,71 @@
 
 def project(extent, rows, tiles, place_ref, *refs):
     tile_refs, weight_refs = refs[:tiles], refs[tiles : tiles + 4]
-    gain_ref = refs[tiles + 4]
-    key_ref, value_ref, query_ref, gate_ref, chain_ref, stack = refs[tiles + 5 :]
+    gain_ref, chain_ref, chain_gain_ref, open_ref = refs[tiles + 4 : tiles + 8]
+    value_ref, gate_ref, score_ref, stack, key_rows, query = refs[tiles + 8 :]
     lines = rows * extent
-    slots = chain_ref.shape[0]
+    half = extent // 2
+    heads = FOCUS_NUMBER
+    local_heads = heads // 4
+    slots = place_ref.shape[0]
+    width = gate_ref.shape[1]
+    group = lax.axis_index("ch")
     for m in range(tiles):
         stack[m] = tile_refs[m][...]
     gain = gain_ref[...]
     weights = [
         jnp.concatenate([ref[kind] for ref in weight_refs], axis=0) for kind in range(4)
     ]
+    key_chain = []
     for k in range(slots):
         place = place_ref[k, 0]
         tile = stack[place, 0:lines, :].astype(jnp.float32)
-        chain_ref[k] = stack[place, lines : lines + 8, 0:128].astype(jnp.float32)
+        key_chain.append(stack[place, lines : lines + 8, 0:128].astype(jnp.float32)[0:1])
         normed = standardized(tile, gain).astype(jnp.bfloat16)
         if k == 0:
-            put(query_ref, dot(normed, weights[0], BOTH_LAST).astype(jnp.bfloat16).astype(jnp.float32))
+            asked = dot(normed, weights[0], BOTH_LAST).astype(jnp.bfloat16)
+            put(query, asked.astype(jnp.float32))
             gate_ref[...] = dot(normed, weights[3], BOTH_LAST).astype(jnp.bfloat16)
         keys = dot(normed, weights[1], BOTH_LAST).astype(jnp.bfloat16)
         values = dot(normed, weights[2], BOTH_LAST).astype(jnp.bfloat16)
         for s in range(rows):
             part = slice(s * extent, (s + 1) * extent)
-            key_ref[s, k * extent : (k + 1) * extent, :] = keys[part]
+            key_rows[s, k * extent : (k + 1) * extent, :] = keys[part]
             value_ref[s, k * extent : (k + 1) * extent, :] = values[part]
+    low = lax.broadcasted_iota(jnp.int32, (half, 128), 1) < extent
+    head_lane = lane_block((half, width), FOCUS_BREADTH)
+    is_open, chain = [], []
+    for k in range(0, slots, 2):
+        is_open.append(jnp.where(low, open_ref[k : k + 1, :], open_ref[k + 1 : k + 2, :]) > 0.0)
+        chain.append(jnp.where(low[0:1], key_chain[k], key_chain[k + 1]))
+    for p in range(2):
+        same = [
+            (chain_ref[p * half : (p + 1) * half, :] == one).astype(jnp.float32)
+            for one in chain
+        ]
+        for s in range(rows):
+            asked = take_every(query, s * extent + p, half, 2)
+            asked = jnp.concatenate(
+                [jnp.where(head_lane == h, asked, 0.0) for h in range(heads)], axis=0
+            ).astype(jnp.bfloat16)
+            scores = dot(asked, key_rows[s], BOTH_LAST) * FOCUS_BREADTH ** (-0.5)
+            for h in range(heads):
+                index = (group ^ (h // local_heads)) * local_heads + h % local_heads
+                gain_row = chain_gain_ref[pl.ds(index, 1), :]
+                rows_h = slice(h * half, (h + 1) * half)
+                for q in range(slots // 2):
+                    lanes = slice(q * 128, (q + 1) * 128)
+                    score_ref[s, p, rows_h, lanes] = jnp.where(
+                        is_open[q], scores[rows_h, lanes] + gain_row * same[q], MASKED
+                    )
 
 
 def attention(extent, rows, *refs):
-    key_ref, value_ref, query_ref, gate_ref, key_chain_ref, tile_ref = refs[:6]
-    weight_refs = refs[6:10]
-    bias_refs = refs[10:14]
-    chain_ref, chain_gain_ref, gain_ref, open_ref = refs[14:18]
-    row_ref, right_ref, pair, bias, attended = refs[18:]
-    slots = key_chain_ref.shape[0]
+    value_ref, gate_ref, score_ref, tile_ref = refs[:4]
+    weight_refs, bias_refs = refs[4:8], refs[8:12]
+    gain_ref = refs[12]
+    row_ref, right_ref, pair, bias, attended = refs[13:]
+    slots = pair.shape[0]
     heads = FOCUS_NUMBER
     local_heads = heads // 4
     width = row_ref.shape[1]
@@ -521,39 +553,24 @@
 
     low = lax.broadcasted_iota(jnp.int32, (half, 128), 1) < extent
     for k in range(0, slots, 2):
-        chain = jnp.where(low[0:1], key_chain_ref[k, 0:1], key_chain_ref[k + 1, 0:1])
-        is_open = jnp.where(low, open_ref[k : k + 1, :], open_ref[k + 1 : k + 2, :]) > 0.0
-        same = [
-            (chain_ref[p * half : (p + 1) * half, :] == chain).astype(jnp.float32)
-            for p in range(2)
-        ]
         lanes = slice((k // 2) * 128, (k // 2 + 1) * 128)
         for h in range(heads):
             rows_h = slice(h * half, (h + 1) * half)
             zero = pair[k, rows_h, :].astype(jnp.float32)
             one = pair[k + 1, rows_h, :].astype(jnp.float32)
-            joined = (
-                jnp.where(low, zero, pltpu.roll(one, extent, 1)),
-                jnp.where(low, pltpu.roll(zero, extent, 1), one),
-            )
-            for p in range(2):
-                value = joined[p] + chain_gain_ref[h : h + 1, :] * same[p]
-                bias[p, rows_h, lanes] = jnp.where(is_open, value, MASKED)
+            bias[0, rows_h, lanes] = jnp.where(low, zero, pltpu.roll(one, extent, 1))
+            bias[1, rows_h, lanes] = jnp.where(low, pltpu.roll(zero, extent, 1), one)
 
     head_lane = lane_block((half, width), FOCUS_BREADTH)
     for s in range(rows):
         for p in range(2):
-            asked = take_every(query_ref, s * extent + p, half, 2)
-            asked = jnp.concatenate(
-                [jnp.where(head_lane == h, asked, 0.0) for h in range(heads)], axis=0
-            ).astype(jnp.bfloat16)
-            scores = dot(asked, key_ref[s], BOTH_LAST) * FOCUS_BREADTH ** (-0.5)
             parts = []
             for h in range(heads):
                 index = (group ^ (h // local_heads)) * local_heads + h % local_heads
                 start = pl.multiple_of(index * half, half)
                 parts.append(
-                    scores[h * half : (h + 1) * half] + bias[p, pl.ds(start, half), :]
+                    score_ref[s, p, h * half : (h + 1) * half, :]
+                    + bias[p, pl.ds(start, half), :]
                 )
             scores = jnp.concatenate(parts, axis=0)
             peak = jnp.max(scores, axis=1, keepdims=True)
@@ -882,18 +899,28 @@
         2_000_000,
     )
 
-    keys, values, query, gates, key_chain = call(
+    values, gates, scores = call(
         functools.partial(project, extent, rows, tiles),
         (
             short(rows, slots * extent, width),
-            short(rows, slots * extent, width),
-            full(block, lines, 128),
             short(lines, width),
-            full(slots, 8, 128),
+            full(rows, 2, heads * half, slots * extent),
         ),
-        (place, *tile_pieces, *weight_pieces, gain_one),
-        [spec()] * (tiles + 6),
-        [pltpu.VMEM((tiles, lines + 8, width), jnp.bfloat16)],
+        (
+            place,
+            *tile_pieces,
+            *weight_pieces,
+            gain_one,
+            chain_column,
+            chain_gain,
+            present,
+        ),
+        [spec()] * (tiles + 9),
+        [
+            pltpu.VMEM((tiles, lines + 8, width), jnp.bfloat16),
+            pltpu.VMEM((rows, slots * extent, width), jnp.bfloat16),
+            vmem(block, lines, 128),
+        ],
         200_000_000,
         2_000_000,
     )
@@ -901,20 +928,15 @@
         functools.partial(attention, extent, rows),
         (short(lines, width), short(features, lines)),
         (
-            keys,
             values,
-            query,
             gates,
-            key_chain,
+            scores,
             tile_piece,
             *weight_pieces,
             *bias_pieces,
-            chain_column,
-            chain_gain,
             gain_two,
-            present,
         ),
-        [spec()] * 18,
+        [spec()] * 13,
         [
             pltpu.VMEM((slots, heads * half, 128), jnp.bfloat16),
             vmem(2, heads * half, slots * extent),

time: 55.8 us -> 51.9 us (0.930)
  waiting for transfers between devices: 17.6 us -> 13.3 us
  starting transfers between devices: 28 us -> 28.6 us
    ppermute x25, waiting for transfers between devices: 17.6 us -> 13.3 us  [flip(): return lax.ppermute(values, axis, [(i, i ^ bits) for i in range(size)])]
    ppermute x25, starting transfers between devices: 28 us -> 28.6 us  [flip(): return lax.ppermute(values, axis, [(i, i ^ bits) for i in range(size)])]
  transfers between devices with their start and end apart: 25 -> 25, of which waited for: 9 -> 7; matrix products, arithmetic and copies ran while one was open for 0% -> 0% of each run, Pallas kernels for 7% -> 8%
where the time goes in v2:
time: 51.9 us; the launch traced here: 51.7 us
  starting transfers between devices  28.6 us (55%)
  waiting for transfers between devices  13.3 us (26%)
  Pallas kernels  9.05 us (17%)
  between operations  0.79 us (2%)
    ppermute x25, starting transfers between devices, flip(): return lax.ppermute(values, axis, [(i, i ^ bits) for i in range(size)])  28.6 us
    ppermute x25, waiting for transfers between devices, flip(): return lax.ppermute(values, axis, [(i, i ^ bits) for i in range(size)])  13.3 us
    pallas_call x10, Pallas kernels, call(): pl.pallas_call(body, out_shape=out, in_specs=specs, out_specs=out_specs,...  7.44 us
    pallas_call x1, Pallas kernels, small(): pl.pallas_call(functools.partial(pair_update, extent, rows, 1.0 / sequenc...  1.61 us
  transfers between devices with their start and end apart: 25, of which 7 were waited for; matrix products, arithmetic and copies ran while one was open for 0% of the time, Pallas kernels for 8%

profile of v2, /device:TPU:0, one launch (start us, length us, event | category | flops | bytes accessed | tf_op | source)
XLA Modules:
  0.0 51.7 jit_solution(15946508142631404194)
XLA Ops:
  0.6 1.6 %shard_map.167 = (bf16[136,256]{1,0:T(8,128)(2,1)S(1)}, bf16[8,64,256]{2,1,0:T(8,128)(2,1)S(1)}, bf16[4,32,4096]{2,1,0:T(8,128)(2,1)S(1)}, bf16[32,32]{1,0:T(8,1...) custom-call(bf16[8,64,256]{2,1,0:T(8,128)(2,1)} %refs_0_.1, ...), custom_call_target="tpu_custom_call" | custom-call | flops 1000000 | bytes 3000000 | tf_op jit(solution)/shard_map/pallas_call | solution.py:292
  2.3 0.4 shard_map.170
  2.7 0.6 %collective-permute-start.10 = (f32[2,8,5248]{2,1,0:T(8,128)S(1)}, f32[2,8,5248]{2,1,0:T(8,128)S(1)}, u32[]{:S(2)}, u32[]{:S(2)}) collective-permute-start(f32[2,8,5248]{2,1,0:T(8,128)S(1)} %shard_map.170), channel_id=1, source_target_pairs={{0,1},{1,0},{2,3},{3,2},{4,5},{5,4},{6,7},{7,6},{8,9},{9,8},{10,11... | collective-permute-start | bytes 1007624 | tf_op jit(solution)/shard_map/ppermute | solution.py:226
  3.3 2.5 %collective-permute-start.8 = (bf16[8,64,256]{2,1,0:T(8,128)(2,1)S(1)}, bf16[8,64,256]{2,1,0:T(8,128)(2,1)S(1)}, u32[]{:S(2)}, u32[]{:S(2)}) collective-permute-start(bf16[8,64,256]{2,1,0:T(8,128)(2,1)S(1)} %get-tuple-element.25.refs_8_.refs_4_.refs_0_), channel_id=1, source_target_pairs={{0,2},{1,3},{2,0},{3,1},{4,6},{5,7},{6,4},{7,5},{8,10},{9,11},{10,... | collective-permute-start | bytes 786440 | tf_op jit(solution)/shard_map/ppermute | solution.py:226
  5.8 0.4 shard_map.169.own_ref
  6.2 0.1 shard_map.171
  6.4 1.2 %collective-permute-start.11 = (f32[8,5248]{1,0:T(8,128)S(1)}, f32[8,5248]{1,0:T(8,128)S(1)}, u32[]{:S(2)}, u32[]{:S(2)}) collective-permute-start(f32[8,5248]{1,0:T(8,128)S(1)} %get-tuple-element.36), channel_id=1, source_target_pairs={{0,2},{1,3},{2,0},{3,1},{4,6},{5,7},{6,4},{7,5},{8,10},{9,11},{10,... | collective-permute-start | bytes 503816 | tf_op jit(solution)/shard_map/ppermute | solution.py:226
  7.5 3.6 %collective-permute-start.5 = (bf16[136,256]{1,0:T(8,128)(2,1)S(1)}, bf16[136,256]{1,0:T(8,128)(2,1)S(1)}, u32[]{:S(2)}, u32[]{:S(2)}) collective-permute-start(bf16[136,256]{1,0:T(8,128)(2,1)S(1)} %get-tuple-element.24.refs_0_.refs_3_), channel_id=1, source_target_pairs={{0,24},{4,28},{8,16},{12,20},{16,8},{20,12},{24,0},{28,4},{1,25},{... | collective-permute-start | bytes 208904 | tf_op jit(solution)/shard_map/ppermute | solution.py:226
  11.2 0.0 collective-permute-start.7
  11.2 1.8 %collective-permute-done.8.refs_10_.refs_6_.refs_2_ = bf16[8,64,256]{2,1,0:T(8,128)(2,1)S(1)} collective-permute-done((bf16[8,64,256]{2,1,0:T(8,128)(2,1)S(1)}, bf16[8,64,256]{2,1,0:T(8,128)(2,1)S(1)}, u32[]{:S(2)}, u32[]{:S(2)}) %collective-permute-start.8) | collective-permute-done | bytes 262176 | tf_op jit(solution)/shard_map/ppermute | solution.py:226
  13.0 0.0 collective-permute-start.9
  13.0 3.1 %collective-permute-start.3 = (bf16[136,256]{1,0:T(8,128)(2,1)S(1)}, bf16[136,256]{1,0:T(8,128)(2,1)S(1)}, u32[]{:S(2)}, u32[]{:S(2)}) collective-permute-start(bf16[136,256]{1,0:T(8,128)(2,1)S(1)} %get-tuple-element.24.refs_0_.refs_3_), channel_id=1, source_target_pairs={{0,16},{4,20},{8,24},{12,28},{16,0},{20,4},{24,8},{28,12},{1,17},{... | collective-permute-start | bytes 208904 | tf_op jit(solution)/shard_map/ppermute | solution.py:226
  16.1 0.0 collective-permute-done.5.refs_6_
  16.1 1.6 %collective-permute-start.1 = (bf16[136,256]{1,0:T(8,128)(2,1)S(1)}, bf16[136,256]{1,0:T(8,128)(2,1)S(1)}, u32[]{:S(2)}, u32[]{:S(2)}) collective-permute-start(bf16[136,256]{1,0:T(8,128)(2,1)S(1)} %get-tuple-element.24.refs_0_.refs_3_), channel_id=1, source_target_pairs={{0,8},{4,12},{8,0},{12,4},{16,24},{20,28},{24,16},{28,20},{1,9},{5... | collective-permute-start | bytes 208904 | tf_op jit(solution)/shard_map/ppermute | solution.py:226
  17.7 2.7 %collective-permute-done.3.refs_4_ = bf16[136,256]{1,0:T(8,128)(2,1)S(1)} collective-permute-done((bf16[136,256]{1,0:T(8,128)(2,1)S(1)}, bf16[136,256]{1,0:T(8,128)(2,1)S(1)}, u32[]{:S(2)}, u32[]{:S(2)}) %collective-permute-start.3) | collective-permute-done | bytes 69664 | tf_op jit(solution)/shard_map/ppermute | solution.py:226
  20.3 1.6 %collective-permute-start = (bf16[136,256]{1,0:T(8,128)(2,1)S(1)}, bf16[136,256]{1,0:T(8,128)(2,1)S(1)}, u32[]{:S(2)}, u32[]{:S(2)}) collective-permute-start(bf16[136,256]{1,0:T(8,128)(2,1)S(1)} %get-tuple-element.24.refs_0_.refs_3_), channel_id=1, source_target_pairs={{0,4},{4,0},{8,12},{12,8},{16,20},{20,16},{24,28},{28,24},{1,5},{5... | collective-permute-start | bytes 208904 | tf_op jit(solution)/shard_map/ppermute | solution.py:226
  22.0 0.4 collective-permute-start.6
  22.4 0.0 collective-permute-done.11.far_ref
  22.4 1.6 %collective-permute-start.4 = (bf16[136,256]{1,0:T(8,128)(2,1)S(1)}, bf16[136,256]{1,0:T(8,128)(2,1)S(1)}, u32[]{:S(2)}, u32[]{:S(2)}) collective-permute-start(bf16[136,256]{1,0:T(8,128)(2,1)S(1)} %collective-permute-done.3.refs_4_), channel_id=1, source_target_pairs={{0,4},{4,0},{8,12},{12,8},{16,20},{20,16},{24,28},{28,24},{1,5},{5... | collective-permute-start | bytes 208904 | tf_op jit(solution)/shard_map/ppermute | solution.py:226
  24.0 0.2 shard_map.172.refs_8_
  24.2 1.2 %collective-permute-done.refs_1_ = bf16[136,256]{1,0:T(8,128)(2,1)S(1)} collective-permute-done((bf16[136,256]{1,0:T(8,128)(2,1)S(1)}, bf16[136,256]{1,0:T(8,128)(2,1)S(1)}, u32[]{:S(2)}, u32[]{:S(2)}) %collective-permute-start) | collective-permute-done | bytes 69664 | tf_op jit(solution)/shard_map/ppermute | solution.py:226
  25.4 1.2 %collective-permute-start.13 = (bf16[256,128]{1,0:T(8,128)(2,1)S(1)}, bf16[256,128]{1,0:T(8,128)(2,1)S(1)}, u32[]{:S(2)}, u32[]{:S(2)}) collective-permute-start(bf16[256,128]{1,0:T(8,128)(2,1)S(1)} %shard_map.172.refs_8_), channel_id=1, source_target_pairs={{0,2},{1,3},{2,0},{3,1},{4,6},{5,7},{6,4},{7,5},{8,10},{9,11},{10,... | collective-permute-start | bytes 196616 | tf_op jit(solution)/shard_map/ppermute | solution.py:226
  26.6 0.0 collective-permute-done.6.refs_7_
  26.6 1.2 %collective-permute-start.2 = (bf16[136,256]{1,0:T(8,128)(2,1)S(1)}, bf16[136,256]{1,0:T(8,128)(2,1)S(1)}, u32[]{:S(2)}, u32[]{:S(2)}) collective-permute-start(bf16[136,256]{1,0:T(8,128)(2,1)S(1)} %collective-permute-done.1.refs_2_), channel_id=1, source_target_pairs={{0,4},{4,0},{8,12},{12,8},{16,20},{20,16},{24,28},{28,24},{1,5},{5... | collective-permute-start | bytes 208904 | tf_op jit(solution)/shard_map/ppermute | solution.py:226
  27.8 0.0 collective-permute-done.4.refs_5_
  27.8 0.0 collective-permute-start.12
  27.8 1.9 %collective-permute-done.13.refs_10_ = bf16[256,128]{1,0:T(8,128)(2,1)S(1)} collective-permute-done((bf16[256,128]{1,0:T(8,128)(2,1)S(1)}, bf16[256,128]{1,0:T(8,128)(2,1)S(1)}, u32[]{:S(2)}, u32[]{:S(2)}) %collective-permute-start.13) | collective-permute-done | bytes 65568 | tf_op jit(solution)/shard_map/ppermute | solution.py:226
  29.7 0.0 collective-permute-start.14
  29.7 1.3 %collective-permute-done.2.refs_3_ = bf16[136,256]{1,0:T(8,128)(2,1)S(1)} collective-permute-done((bf16[136,256]{1,0:T(8,128)(2,1)S(1)}, bf16[136,256]{1,0:T(8,128)(2,1)S(1)}, u32[]{:S(2)}, u32[]{:S(2)}) %collective-permute-start.2) | collective-permute-done | bytes 69664 | tf_op jit(solution)/shard_map/ppermute | solution.py:226
  30.9 0.0 collective-permute-done.9.refs_11_.refs_7_.refs_3_
  30.9 1.1 %shard_map.168 = (bf16[2,256,256]{2,1,0:T(8,128)(2,1)S(1)}, bf16[128,256]{1,0:T(8,128)(2,1)S(1)}, f32[2,2,256,256]{3,2,1,0:T(8,128)S(1)}) custom-call(s32[4,128]{1,0:T(4,128)S(1)} %get-tuple-element.23.place_ref, bf16[136,256]{1,0:T(8,128)(2,1)S(1)} %get-tuple-element.24.refs_0_.refs_3_, bf16[136,256]{1,0:T(8,128)(2,1)S(1)} %collective-permute-done.refs_1_, ...), custom_call_target="tpu_custom_call" | custom-call | flops 200000000 | bytes 2000000 | tf_op jit(solution)/shard_map/pallas_call | solution.py:292
  32.1 0.0 collective-permute-done.14.refs_11_
  32.1 1.1 %shard_map.173 = (bf16[128,256]{1,0:T(8,128)(2,1)S(1)}, bf16[32,128]{1,0:T(8,128)(2,1)S(1)}) custom-call(bf16[2,256,256]{2,1,0:T(8,128)(2,1)S(1)} %get-tuple-element.30.refs_0_, bf16[128,256]{1,0:T(8,128)(2,1)S(1)} %get-tuple-element.31.refs_1_, f32[2,2,256,256]{3,2,1,0:T(8,128)S(1)} %get-tuple-element.32.refs_2_, ...), custom_call_target="tpu_custom_call" | custom-call | flops 600000000 | bytes 3000000 | tf_op jit(solution)/shard_map/pallas_call | solution.py:292
  33.2 3.9 %collective-permute-start.20 = (bf16[32,128]{1,0:T(8,128)(2,1)S(1)}, bf16[32,128]{1,0:T(8,128)(2,1)S(1)}, u32[]{:S(2)}, u32[]{:S(2)}) collective-permute-start(bf16[32,128]{1,0:T(8,128)(2,1)S(1)} %get-tuple-element.43), channel_id=1, source_target_pairs={{0,24},{4,28},{8,16},{12,20},{16,8},{20,12},{24,0},{28,4},{1,25},{... | collective-permute-start | bytes 24584 | tf_op jit(solution)/shard_map/ppermute | solution.py:226
  37.1 0.6 %collective-permute-start.18 = (bf16[32,128]{1,0:T(8,128)(2,1)S(1)}, bf16[32,128]{1,0:T(8,128)(2,1)S(1)}, u32[]{:S(2)}, u32[]{:S(2)}) collective-permute-start(bf16[32,128]{1,0:T(8,128)(2,1)S(1)} %get-tuple-element.43), channel_id=1, source_target_pairs={{0,8},{4,12},{8,0},{12,4},{16,24},{20,28},{24,16},{28,20},{1,9},{5... | collective-permute-start | bytes 24584 | tf_op jit(solution)/shard_map/ppermute | solution.py:226
  37.7 0.0 collective-permute-start.17
  37.8 1.5 %collective-permute-start.16 = (bf16[128,256]{1,0:T(8,128)(2,1)S(1)}, bf16[128,256]{1,0:T(8,128)(2,1)S(1)}, u32[]{:S(2)}, u32[]{:S(2)}) collective-permute-start(bf16[128,256]{1,0:T(8,128)(2,1)S(1)} %get-tuple-element.38.refs_0_), channel_id=1, source_target_pairs={{0,2},{1,3},{2,0},{3,1},{4,6},{5,7},{6,4},{7,5},{8,10},{9,11},{10,... | collective-permute-start | bytes 196616 | tf_op jit(solution)/shard_map/ppermute | solution.py:226
  39.3 0.4 collective-permute-start.15
  39.6 2.1 %collective-permute-done.19 = bf16[32,128]{1,0:T(8,128)(2,1)S(1)} collective-permute-done((bf16[32,128]{1,0:T(8,128)(2,1)S(1)}, bf16[32,128]{1,0:T(8,128)(2,1)S(1)}, u32[]{:S(2)}, u32[]{:S(2)}) %collective-permute-start.19) | collective-permute-done | bytes 8224 | tf_op jit(solution)/shard_map/ppermute | solution.py:226
  41.7 1.6 %collective-permute-start.21 = (bf16[4,32,128]{2,1,0:T(8,128)(2,1)S(1)}, bf16[4,32,128]{2,1,0:T(8,128)(2,1)S(1)}, u32[]{:S(2)}, u32[]{:S(2)}) collective-permute-start(bf16[4,32,128]{2,1,0:T(8,128)(2,1)S(1)} %pad_maximum_fusion.even_ref), channel_id=1, source_target_pairs={{0,4},{4,0},{8,12},{12,8},{16,20},{20,16},{24,28},{28,24},{1,5},{5... | collective-permute-start | bytes 98312 | tf_op jit(solution)/shard_map/ppermute | solution.py:226
  43.3 2.4 %collective-permute-done.21.odd_ref = bf16[4,32,128]{2,1,0:T(8,128)(2,1)S(1)} collective-permute-done((bf16[4,32,128]{2,1,0:T(8,128)(2,1)S(1)}, bf16[4,32,128]{2,1,0:T(8,128)(2,1)S(1)}, u32[]{:S(2)}, u32[]{:S(2)}) %collective-permute-start.21) | collective-permute-done | bytes 32800 | tf_op jit(solution)/shard_map/ppermute | solution.py:226
  45.7 0.1 shard_map.176.refs_0_
  45.8 0.1 collective-permute-start.24
  45.8 1.6 %collective-permute-start.23 = (bf16[4,32,128]{2,1,0:T(8,128)(2,1)S(1)}, bf16[4,32,128]{2,1,0:T(8,128)(2,1)S(1)}, u32[]{:S(2)}, u32[]{:S(2)}) collective-permute-start(bf16[4,32,128]{2,1,0:T(8,128)(2,1)S(1)} %shard_map.176.refs_0_), channel_id=1, source_target_pairs={{0,2},{1,3},{2,0},{3,1},{4,6},{5,7},{6,4},{7,5},{8,10},{9,11},{10,... | collective-permute-start | bytes 98312 | tf_op jit(solution)/shard_map/ppermute | solution.py:226
  47.4 0.3 collective-permute-start.22
  47.7 0.4 shard_map.174.refs_6_
  48.2 1.9 %shard_map.175 = (bf16[1024,512]{1,0:T(8,128)(2,1)S(1)}, bf16[8,64,256]{2,1,0:T(8,128)(2,1)}) custom-call(bf16[128,256]{1,0:T(8,128)(2,1)S(1)} %get-tuple-element.38.refs_0_, bf16[128,256]{1,0:T(8,128)(2,1)S(1)} %collective-permute-done.15.refs_1_, bf16[128,256]{1,0:T(8,128)(2,1)S(1)} %collective-permute-done.16.refs_2_, ...), custom_call_target="tpu_custom_call" | custom-call | flops 300000000 | bytes 3000000 | tf_op jit(solution)/shard_map/pallas_call | solution.py:292
  50.1 1.6 %pair_update.1 = bf16[4,32,4096]{2,1,0:T(8,128)(2,1)} custom-call(f32[4,128]{1,0:T(4,128)S(1)} %get-tuple-element.29.refs_15_.open_ref, bf16[1024,512]{1,0:T(8,128)(2,1)S(1)} %get-tuple-element.41.table_ref, bf16[4,32,4096]{2,1,0:T(8,128)(2,1)S(1)} %get-tuple-element.34.pair_ref, f32[32,128]{1,0:T(8,128)S(1)} %get-tuple-element.42.offset_ref, ...), custom_call_target="tpu_custom_call" | custom-call | flops 600000000 | bytes 3000000 | tf_op jit(solution)/shard_map/pair_update/pallas_call | solution.py:978
  (14 shorter events, 0.0 us)
Async XLA Ops:
  2.7 3.5 %collective-permute-start.10 = (f32[2,8,5248]{2,1,0:T(8,128)S(1)}, f32[2,8,5248]{2,1,0:T(8,128)S(1)}, u32[]{:S(2)}, u32[]{:S(2)}) collective-permute-start(f32[2,8,5248]{2,1,0:T(8,128)S(1)} %shard_map.170), channel_id=1, source_target_pairs={{0,1},{1,0},{2,3},{3,2},{4,5},{5,4},{6,7},{7,6},{8,9},{9,8},{10,11... | collective-permute-start | bytes 1007624 | tf_op jit(solution)/shard_map/ppermute | solution.py:226
  3.3 9.7 %collective-permute-start.8 = (bf16[8,64,256]{2,1,0:T(8,128)(2,1)S(1)}, bf16[8,64,256]{2,1,0:T(8,128)(2,1)S(1)}, u32[]{:S(2)}, u32[]{:S(2)}) collective-permute-start(bf16[8,64,256]{2,1,0:T(8,128)(2,1)S(1)} %get-tuple-element.25.refs_8_.refs_4_.refs_0_), channel_id=1, source_target_pairs={{0,2},{1,3},{2,0},{3,1},{4,6},{5,7},{6,4},{7,5},{8,10},{9,11},{10,... | collective-permute-start | bytes 786440 | tf_op jit(solution)/shard_map/ppermute | solution.py:226
  6.4 16.0 %collective-permute-start.11 = (f32[8,5248]{1,0:T(8,128)S(1)}, f32[8,5248]{1,0:T(8,128)S(1)}, u32[]{:S(2)}, u32[]{:S(2)}) collective-permute-start(f32[8,5248]{1,0:T(8,128)S(1)} %get-tuple-element.36), channel_id=1, source_target_pairs={{0,2},{1,3},{2,0},{3,1},{4,6},{5,7},{6,4},{7,5},{8,10},{9,11},{10,... | collective-permute-start | bytes 503816 | tf_op jit(solution)/shard_map/ppermute | solution.py:226
  7.5 8.6 %collective-permute-start.5 = (bf16[136,256]{1,0:T(8,128)(2,1)S(1)}, bf16[136,256]{1,0:T(8,128)(2,1)S(1)}, u32[]{:S(2)}, u32[]{:S(2)}) collective-permute-start(bf16[136,256]{1,0:T(8,128)(2,1)S(1)} %get-tuple-element.24.refs_0_.refs_3_), channel_id=1, source_target_pairs={{0,24},{4,28},{8,16},{12,20},{16,8},{20,12},{24,0},{28,4},{1,25},{... | collective-permute-start | bytes 208904 | tf_op jit(solution)/shard_map/ppermute | solution.py:226
  11.2 19.8 %collective-permute-start.7 = (bf16[8,64,256]{2,1,0:T(8,128)(2,1)S(1)}, bf16[8,64,256]{2,1,0:T(8,128)(2,1)S(1)}, u32[]{:S(2)}, u32[]{:S(2)}) collective-permute-start(bf16[8,64,256]{2,1,0:T(8,128)(2,1)S(1)} %get-tuple-element.25.refs_8_.refs_4_.refs_0_), channel_id=1, source_target_pairs={{0,1},{1,0},{2,3},{3,2},{4,5},{5,4},{6,7},{7,6},{8,9},{9,8},{10,11... | collective-permute-start | bytes 786440 | tf_op jit(solution)/shard_map/ppermute | solution.py:226
  13.0 18.0 %collective-permute-start.9 = (bf16[8,64,256]{2,1,0:T(8,128)(2,1)S(1)}, bf16[8,64,256]{2,1,0:T(8,128)(2,1)S(1)}, u32[]{:S(2)}, u32[]{:S(2)}) collective-permute-start(bf16[8,64,256]{2,1,0:T(8,128)(2,1)S(1)} %collective-permute-done.8.refs_10_.refs_6_.refs_2_), channel_id=1, source_target_pairs={{0,1},{1,0},{2,3},{3,2},{4,5},{5,4},{6,7},{7,6},{8,9},{9,8},{10,11... | collective-permute-start | bytes 786440 | tf_op jit(solution)/shard_map/ppermute | solution.py:226
  13.0 7.4 %collective-permute-start.3 = (bf16[136,256]{1,0:T(8,128)(2,1)S(1)}, bf16[136,256]{1,0:T(8,128)(2,1)S(1)}, u32[]{:S(2)}, u32[]{:S(2)}) collective-permute-start(bf16[136,256]{1,0:T(8,128)(2,1)S(1)} %get-tuple-element.24.refs_0_.refs_3_), channel_id=1, source_target_pairs={{0,16},{4,20},{8,24},{12,28},{16,0},{20,4},{24,8},{28,12},{1,17},{... | collective-permute-start | bytes 208904 | tf_op jit(solution)/shard_map/ppermute | solution.py:226
  16.1 5.9 %collective-permute-start.1 = (bf16[136,256]{1,0:T(8,128)(2,1)S(1)}, bf16[136,256]{1,0:T(8,128)(2,1)S(1)}, u32[]{:S(2)}, u32[]{:S(2)}) collective-permute-start(bf16[136,256]{1,0:T(8,128)(2,1)S(1)} %get-tuple-element.24.refs_0_.refs_3_), channel_id=1, source_target_pairs={{0,8},{4,12},{8,0},{12,4},{16,24},{20,28},{24,16},{28,20},{1,9},{5... | collective-permute-start | bytes 208904 | tf_op jit(solution)/shard_map/ppermute | solution.py:226
  20.3 5.1 %collective-permute-start = (bf16[136,256]{1,0:T(8,128)(2,1)S(1)}, bf16[136,256]{1,0:T(8,128)(2,1)S(1)}, u32[]{:S(2)}, u32[]{:S(2)}) collective-permute-start(bf16[136,256]{1,0:T(8,128)(2,1)S(1)} %get-tuple-element.24.refs_0_.refs_3_), channel_id=1, source_target_pairs={{0,4},{4,0},{8,12},{12,8},{16,20},{20,16},{24,28},{28,24},{1,5},{5... | collective-permute-start | bytes 208904 | tf_op jit(solution)/shard_map/ppermute | solution.py:226
  22.0 4.6 %collective-permute-start.6 = (bf16[136,256]{1,0:T(8,128)(2,1)S(1)}, bf16[136,256]{1,0:T(8,128)(2,1)S(1)}, u32[]{:S(2)}, u32[]{:S(2)}) collective-permute-start(bf16[136,256]{1,0:T(8,128)(2,1)S(1)} %collective-permute-done.5.refs_6_), channel_id=1, source_target_pairs={{0,4},{4,0},{8,12},{12,8},{16,20},{20,16},{24,28},{28,24},{1,5},{5... | collective-permute-start | bytes 208904 | tf_op jit(solution)/shard_map/ppermute | solution.py:226
  22.4 5.4 %collective-permute-start.4 = (bf16[136,256]{1,0:T(8,128)(2,1)S(1)}, bf16[136,256]{1,0:T(8,128)(2,1)S(1)}, u32[]{:S(2)}, u32[]{:S(2)}) collective-permute-start(bf16[136,256]{1,0:T(8,128)(2,1)S(1)} %collective-permute-done.3.refs_4_), channel_id=1, source_target_pairs={{0,4},{4,0},{8,12},{12,8},{16,20},{20,16},{24,28},{28,24},{1,5},{5... | collective-permute-start | bytes 208904 | tf_op jit(solution)/shard_map/ppermute | solution.py:226
  25.4 4.3 %collective-permute-start.13 = (bf16[256,128]{1,0:T(8,128)(2,1)S(1)}, bf16[256,128]{1,0:T(8,128)(2,1)S(1)}, u32[]{:S(2)}, u32[]{:S(2)}) collective-permute-start(bf16[256,128]{1,0:T(8,128)(2,1)S(1)} %shard_map.172.refs_8_), channel_id=1, source_target_pairs={{0,2},{1,3},{2,0},{3,1},{4,6},{5,7},{6,4},{7,5},{8,10},{9,11},{10,... | collective-permute-start | bytes 196616 | tf_op jit(solution)/shard_map/ppermute | solution.py:226
  26.6 4.3 %collective-permute-start.2 = (bf16[136,256]{1,0:T(8,128)(2,1)S(1)}, bf16[136,256]{1,0:T(8,128)(2,1)S(1)}, u32[]{:S(2)}, u32[]{:S(2)}) collective-permute-start(bf16[136,256]{1,0:T(8,128)(2,1)S(1)} %collective-permute-done.1.refs_2_), channel_id=1, source_target_pairs={{0,4},{4,0},{8,12},{12,8},{16,20},{20,16},{24,28},{28,24},{1,5},{5... | collective-permute-start | bytes 208904 | tf_op jit(solution)/shard_map/ppermute | solution.py:226
  27.8 4.3 %collective-permute-start.12 = (bf16[256,128]{1,0:T(8,128)(2,1)S(1)}, bf16[256,128]{1,0:T(8,128)(2,1)S(1)}, u32[]{:S(2)}, u32[]{:S(2)}) collective-permute-start(bf16[256,128]{1,0:T(8,128)(2,1)S(1)} %shard_map.172.refs_8_), channel_id=1, source_target_pairs={{0,1},{1,0},{2,3},{3,2},{4,5},{5,4},{6,7},{7,6},{8,9},{9,8},{10,11... | collective-permute-start | bytes 196616 | tf_op jit(solution)/shard_map/ppermute | solution.py:226
  29.7 2.4 %collective-permute-start.14 = (bf16[256,128]{1,0:T(8,128)(2,1)S(1)}, bf16[256,128]{1,0:T(8,128)(2,1)S(1)}, u32[]{:S(2)}, u32[]{:S(2)}) collective-permute-start(bf16[256,128]{1,0:T(8,128)(2,1)S(1)} %collective-permute-done.13.refs_10_), channel_id=1, source_target_pairs={{0,1},{1,0},{2,3},{3,2},{4,5},{5,4},{6,7},{7,6},{8,9},{9,8},{10,11... | collective-permute-start | bytes 196616 | tf_op jit(solution)/shard_map/ppermute | solution.py:226
  33.2 6.1 %collective-permute-start.20 = (bf16[32,128]{1,0:T(8,128)(2,1)S(1)}, bf16[32,128]{1,0:T(8,128)(2,1)S(1)}, u32[]{:S(2)}, u32[]{:S(2)}) collective-permute-start(bf16[32,128]{1,0:T(8,128)(2,1)S(1)} %get-tuple-element.43), channel_id=1, source_target_pairs={{0,24},{4,28},{8,16},{12,20},{16,8},{20,12},{24,0},{28,4},{1,25},{... | collective-permute-start | bytes 24584 | tf_op jit(solution)/shard_map/ppermute | solution.py:226
  37.1 4.5 %collective-permute-start.19 = (bf16[32,128]{1,0:T(8,128)(2,1)S(1)}, bf16[32,128]{1,0:T(8,128)(2,1)S(1)}, u32[]{:S(2)}, u32[]{:S(2)}) collective-permute-start(bf16[32,128]{1,0:T(8,128)(2,1)S(1)} %get-tuple-element.43), channel_id=1, source_target_pairs={{0,16},{4,20},{8,24},{12,28},{16,0},{20,4},{24,8},{28,12},{1,17},{... | collective-permute-start | bytes 24584 | tf_op jit(solution)/shard_map/ppermute | solution.py:226
  37.1 4.5 %collective-permute-start.18 = (bf16[32,128]{1,0:T(8,128)(2,1)S(1)}, bf16[32,128]{1,0:T(8,128)(2,1)S(1)}, u32[]{:S(2)}, u32[]{:S(2)}) collective-permute-start(bf16[32,128]{1,0:T(8,128)(2,1)S(1)} %get-tuple-element.43), channel_id=1, source_target_pairs={{0,8},{4,12},{8,0},{12,4},{16,24},{20,28},{24,16},{28,20},{1,9},{5... | collective-permute-start | bytes 24584 | tf_op jit(solution)/shard_map/ppermute | solution.py:226
  37.7 9.7 %collective-permute-start.17 = (bf16[128,256]{1,0:T(8,128)(2,1)S(1)}, bf16[128,256]{1,0:T(8,128)(2,1)S(1)}, u32[]{:S(2)}, u32[]{:S(2)}) collective-permute-start(bf16[128,256]{1,0:T(8,128)(2,1)S(1)} %get-tuple-element.38.refs_0_), channel_id=1, source_target_pairs={{0,3},{1,2},{2,1},{3,0},{4,7},{5,6},{6,5},{7,4},{8,11},{9,10},{10,... | collective-permute-start | bytes 196616 | tf_op jit(solution)/shard_map/ppermute | solution.py:226
  37.8 10.4 %collective-permute-start.16 = (bf16[128,256]{1,0:T(8,128)(2,1)S(1)}, bf16[128,256]{1,0:T(8,128)(2,1)S(1)}, u32[]{:S(2)}, u32[]{:S(2)}) collective-permute-start(bf16[128,256]{1,0:T(8,128)(2,1)S(1)} %get-tuple-element.38.refs_0_), channel_id=1, source_target_pairs={{0,2},{1,3},{2,0},{3,1},{4,6},{5,7},{6,4},{7,5},{8,10},{9,11},{10,... | collective-permute-start | bytes 196616 | tf_op jit(solution)/shard_map/ppermute | solution.py:226
  39.3 8.9 %collective-permute-start.15 = (bf16[128,256]{1,0:T(8,128)(2,1)S(1)}, bf16[128,256]{1,0:T(8,128)(2,1)S(1)}, u32[]{:S(2)}, u32[]{:S(2)}) collective-permute-start(bf16[128,256]{1,0:T(8,128)(2,1)S(1)} %get-tuple-element.38.refs_0_), channel_id=1, source_target_pairs={{0,1},{1,0},{2,3},{3,2},{4,5},{5,4},{6,7},{7,6},{8,9},{9,8},{10,11... | collective-permute-start | bytes 196616 | tf_op jit(solution)/shard_map/ppermute | solution.py:226
  41.7 4.0 %collective-permute-start.21 = (bf16[4,32,128]{2,1,0:T(8,128)(2,1)S(1)}, bf16[4,32,128]{2,1,0:T(8,128)(2,1)S(1)}, u32[]{:S(2)}, u32[]{:S(2)}) collective-permute-start(bf16[4,32,128]{2,1,0:T(8,128)(2,1)S(1)} %pad_maximum_fusion.even_ref), channel_id=1, source_target_pairs={{0,4},{4,0},{8,12},{12,8},{16,20},{20,16},{24,28},{28,24},{1,5},{5... | collective-permute-start | bytes 98312 | tf_op jit(solution)/shard_map/ppermute | solution.py:226
  45.8 4.3 %collective-permute-start.24 = (bf16[4,32,128]{2,1,0:T(8,128)(2,1)S(1)}, bf16[4,32,128]{2,1,0:T(8,128)(2,1)S(1)}, u32[]{:S(2)}, u32[]{:S(2)}) collective-permute-start(bf16[4,32,128]{2,1,0:T(8,128)(2,1)S(1)} %shard_map.176.refs_0_), channel_id=1, source_target_pairs={{0,3},{1,2},{2,1},{3,0},{4,7},{5,6},{6,5},{7,4},{8,11},{9,10},{10,... | collective-permute-start | bytes 98312 | tf_op jit(solution)/shard_map/ppermute | solution.py:226
  45.8 4.3 %collective-permute-start.23 = (bf16[4,32,128]{2,1,0:T(8,128)(2,1)S(1)}, bf16[4,32,128]{2,1,0:T(8,128)(2,1)S(1)}, u32[]{:S(2)}, u32[]{:S(2)}) collective-permute-start(bf16[4,32,128]{2,1,0:T(8,128)(2,1)S(1)} %shard_map.176.refs_0_), channel_id=1, source_target_pairs={{0,2},{1,3},{2,0},{3,1},{4,6},{5,7},{6,4},{7,5},{8,10},{9,11},{10,... | collective-permute-start | bytes 98312 | tf_op jit(solution)/shard_map/ppermute | solution.py:226
  47.4 2.7 %collective-permute-start.22 = (bf16[4,32,128]{2,1,0:T(8,128)(2,1)S(1)}, bf16[4,32,128]{2,1,0:T(8,128)(2,1)S(1)}, u32[]{:S(2)}, u32[]{:S(2)}) collective-permute-start(bf16[4,32,128]{2,1,0:T(8,128)(2,1)S(1)} %shard_map.176.refs_0_), channel_id=1, source_target_pairs={{0,1},{1,0},{2,3},{3,2},{4,5},{5,4},{6,7},{7,6},{8,9},{9,8},{10,11... | collective-permute-start | bytes 98312 | tf_op jit(solution)/shard_map/ppermute | solution.py:226

commit v3 on v2

--- a/solution.py
+++ b/solution.py
@@ -674,12 +674,13 @@
         table_ref[:, b * 128 : (b + 1) * 128] = spread[b].astype(jnp.bfloat16)
 
 
-def pick(place_ref, even_ref, odd_ref, out_ref):
+def pick(place_ref, *refs):
+    piece_refs = refs[:-2]
+    out_ref, stack = refs[-2:]
+    for m, ref in enumerate(piece_refs):
+        stack[2 * m : 2 * m + 2] = ref[...]
     for k in range(out_ref.shape[0]):
-        place = place_ref[k, 0]
-        even = even_ref[place // 2]
-        odd = odd_ref[place // 2]
-        out_ref[k] = jnp.where(lax.rem(place, 2) == 0, even, odd)
+        out_ref[k] = stack[place_ref[k, 0]]
 
 
 def pair_update(extent, rows, scale, open_ref, table_ref, pair_ref, offset_ref, *refs):
@@ -946,15 +947,15 @@
         3_000_000,
     )
 
-    right_pieces = [right_piece] + [flip(right_piece, "res", bits) for bits in range(2, tiles, 2)]
-    stacked = jnp.stack(right_pieces)
-    turned = flip(stacked, "res", 1)
+    turned = flip(right_piece, "res", 1)
+    stacked = jnp.stack([right_piece, turned])
+    right_pieces = [stacked] + [flip(stacked, "res", bits) for bits in range(2, tiles, 2)]
     picked = call(
         pick,
         short(slots, features, lines),
-        (place, stacked, turned),
-        [spec()] * 3,
-        [],
+        (place, *right_pieces),
+        [spec()] * (1 + tiles // 2),
+        [pltpu.VMEM((tiles, features, lines), jnp.bfloat16)],
         1000,
         200_000,
     )

time: 51.9 us -> 52.4 us (level)
  waiting for transfers between devices: 13.3 us -> 14.9 us
  starting transfers between devices: 28.6 us -> 27.6 us
    ppermute x25, waiting for transfers between devices: 13.3 us -> 14.9 us  [flip(): return lax.ppermute(values, axis, [(i, i ^ bits) for i in range(size)])]
    ppermute x25, starting transfers between devices: 28.6 us -> 27.6 us  [flip(): return lax.ppermute(values, axis, [(i, i ^ bits) for i in range(size)])]
  transfers between devices with their start and end apart: 25 -> 25, of which waited for: 7 -> 9; matrix products, arithmetic and copies ran while one was open for 0% -> 0% of each run, Pallas kernels for 8% -> 8%
where the time goes in v3:
time: 52.4 us; the launch traced here: 52.3 us
  starting transfers between devices  27.6 us (53%)
  waiting for transfers between devices  14.9 us (28%)
  Pallas kernels  9.01 us (17%)
  between operations  0.78 us (1%)
    ppermute x25, starting transfers between devices, flip(): return lax.ppermute(values, axis, [(i, i ^ bits) for i in range(size)])  27.6 us
    ppermute x25, waiting for transfers between devices, flip(): return lax.ppermute(values, axis, [(i, i ^ bits) for i in range(size)])  14.9 us
    pallas_call x10, Pallas kernels, call(): pl.pallas_call(body, out_shape=out, in_specs=specs, out_specs=out_specs,...  7.4 us
    pallas_call x1, Pallas kernels, small(): pl.pallas_call(functools.partial(pair_update, extent, rows, 1.0 / sequenc...  1.62 us
  transfers between devices with their start and end apart: 25, of which 9 were waited for; matrix products, arithmetic and copies ran while one was open for 0% of the time, Pallas kernels for 8%

profile of v3, /device:TPU:0, one launch (start us, length us, event | category | flops | bytes accessed | tf_op | source)
XLA Modules:
  0.0 52.3 jit_solution(13835747910431331548)
XLA Ops:
  0.6 1.6 %shard_map.167 = (bf16[136,256]{1,0:T(8,128)(2,1)S(1)}, bf16[8,64,256]{2,1,0:T(8,128)(2,1)S(1)}, bf16[4,32,4096]{2,1,0:T(8,128)(2,1)S(1)}, bf16[32,32]{1,0:T(8,1...) custom-call(bf16[8,64,256]{2,1,0:T(8,128)(2,1)} %refs_0_.1, ...), custom_call_target="tpu_custom_call" | custom-call | flops 1000000 | bytes 3000000 | tf_op jit(solution)/shard_map/pallas_call | solution.py:292
  2.3 0.4 shard_map.170
  2.7 0.6 %collective-permute-start.10 = (f32[2,8,5248]{2,1,0:T(8,128)S(1)}, f32[2,8,5248]{2,1,0:T(8,128)S(1)}, u32[]{:S(2)}, u32[]{:S(2)}) collective-permute-start(f32[2,8,5248]{2,1,0:T(8,128)S(1)} %shard_map.170), channel_id=1, source_target_pairs={{0,1},{1,0},{2,3},{3,2},{4,5},{5,4},{6,7},{7,6},{8,9},{9,8},{10,11... | collective-permute-start | bytes 1007624 | tf_op jit(solution)/shard_map/ppermute | solution.py:226
  3.3 2.5 %collective-permute-start.8 = (bf16[8,64,256]{2,1,0:T(8,128)(2,1)S(1)}, bf16[8,64,256]{2,1,0:T(8,128)(2,1)S(1)}, u32[]{:S(2)}, u32[]{:S(2)}) collective-permute-start(bf16[8,64,256]{2,1,0:T(8,128)(2,1)S(1)} %get-tuple-element.25.refs_8_.refs_4_.refs_0_), channel_id=1, source_target_pairs={{0,2},{1,3},{2,0},{3,1},{4,6},{5,7},{6,4},{7,5},{8,10},{9,11},{10,... | collective-permute-start | bytes 786440 | tf_op jit(solution)/shard_map/ppermute | solution.py:226
  5.8 0.4 shard_map.169.own_ref
  6.2 0.1 shard_map.171
  6.4 1.2 %collective-permute-start.11 = (f32[8,5248]{1,0:T(8,128)S(1)}, f32[8,5248]{1,0:T(8,128)S(1)}, u32[]{:S(2)}, u32[]{:S(2)}) collective-permute-start(f32[8,5248]{1,0:T(8,128)S(1)} %get-tuple-element.36), channel_id=1, source_target_pairs={{0,2},{1,3},{2,0},{3,1},{4,6},{5,7},{6,4},{7,5},{8,10},{9,11},{10,... | collective-permute-start | bytes 503816 | tf_op jit(solution)/shard_map/ppermute | solution.py:226
  7.5 3.6 %collective-permute-start.5 = (bf16[136,256]{1,0:T(8,128)(2,1)S(1)}, bf16[136,256]{1,0:T(8,128)(2,1)S(1)}, u32[]{:S(2)}, u32[]{:S(2)}) collective-permute-start(bf16[136,256]{1,0:T(8,128)(2,1)S(1)} %get-tuple-element.24.refs_0_.refs_3_), channel_id=1, source_target_pairs={{0,24},{4,28},{8,16},{12,20},{16,8},{20,12},{24,0},{28,4},{1,25},{... | collective-permute-start | bytes 208904 | tf_op jit(solution)/shard_map/ppermute | solution.py:226
  11.2 0.0 collective-permute-start.7
  11.2 1.8 %collective-permute-done.8.refs_10_.refs_6_.refs_2_ = bf16[8,64,256]{2,1,0:T(8,128)(2,1)S(1)} collective-permute-done((bf16[8,64,256]{2,1,0:T(8,128)(2,1)S(1)}, bf16[8,64,256]{2,1,0:T(8,128)(2,1)S(1)}, u32[]{:S(2)}, u32[]{:S(2)}) %collective-permute-start.8) | collective-permute-done | bytes 262176 | tf_op jit(solution)/shard_map/ppermute | solution.py:226
  13.0 0.0 collective-permute-start.9
  13.0 3.1 %collective-permute-start.3 = (bf16[136,256]{1,0:T(8,128)(2,1)S(1)}, bf16[136,256]{1,0:T(8,128)(2,1)S(1)}, u32[]{:S(2)}, u32[]{:S(2)}) collective-permute-start(bf16[136,256]{1,0:T(8,128)(2,1)S(1)} %get-tuple-element.24.refs_0_.refs_3_), channel_id=1, source_target_pairs={{0,16},{4,20},{8,24},{12,28},{16,0},{20,4},{24,8},{28,12},{1,17},{... | collective-permute-start | bytes 208904 | tf_op jit(solution)/shard_map/ppermute | solution.py:226
  16.1 0.0 collective-permute-done.5.refs_6_
  16.1 1.6 %collective-permute-start.1 = (bf16[136,256]{1,0:T(8,128)(2,1)S(1)}, bf16[136,256]{1,0:T(8,128)(2,1)S(1)}, u32[]{:S(2)}, u32[]{:S(2)}) collective-permute-start(bf16[136,256]{1,0:T(8,128)(2,1)S(1)} %get-tuple-element.24.refs_0_.refs_3_), channel_id=1, source_target_pairs={{0,8},{4,12},{8,0},{12,4},{16,24},{20,28},{24,16},{28,20},{1,9},{5... | collective-permute-start | bytes 208904 | tf_op jit(solution)/shard_map/ppermute | solution.py:226
  17.7 2.7 %collective-permute-done.3.refs_4_ = bf16[136,256]{1,0:T(8,128)(2,1)S(1)} collective-permute-done((bf16[136,256]{1,0:T(8,128)(2,1)S(1)}, bf16[136,256]{1,0:T(8,128)(2,1)S(1)}, u32[]{:S(2)}, u32[]{:S(2)}) %collective-permute-start.3) | collective-permute-done | bytes 69664 | tf_op jit(solution)/shard_map/ppermute | solution.py:226
  20.3 1.6 %collective-permute-start = (bf16[136,256]{1,0:T(8,128)(2,1)S(1)}, bf16[136,256]{1,0:T(8,128)(2,1)S(1)}, u32[]{:S(2)}, u32[]{:S(2)}) collective-permute-start(bf16[136,256]{1,0:T(8,128)(2,1)S(1)} %get-tuple-element.24.refs_0_.refs_3_), channel_id=1, source_target_pairs={{0,4},{4,0},{8,12},{12,8},{16,20},{20,16},{24,28},{28,24},{1,5},{5... | collective-permute-start | bytes 208904 | tf_op jit(solution)/shard_map/ppermute | solution.py:226
  22.0 0.4 collective-permute-start.6
  22.4 0.0 collective-permute-done.11.far_ref
  22.4 1.6 %collective-permute-start.4 = (bf16[136,256]{1,0:T(8,128)(2,1)S(1)}, bf16[136,256]{1,0:T(8,128)(2,1)S(1)}, u32[]{:S(2)}, u32[]{:S(2)}) collective-permute-start(bf16[136,256]{1,0:T(8,128)(2,1)S(1)} %collective-permute-done.3.refs_4_), channel_id=1, source_target_pairs={{0,4},{4,0},{8,12},{12,8},{16,20},{20,16},{24,28},{28,24},{1,5},{5... | collective-permute-start | bytes 208904 | tf_op jit(solution)/shard_map/ppermute | solution.py:226
  24.0 0.2 shard_map.172.refs_8_
  24.2 1.2 %collective-permute-done.refs_1_ = bf16[136,256]{1,0:T(8,128)(2,1)S(1)} collective-permute-done((bf16[136,256]{1,0:T(8,128)(2,1)S(1)}, bf16[136,256]{1,0:T(8,128)(2,1)S(1)}, u32[]{:S(2)}, u32[]{:S(2)}) %collective-permute-start) | collective-permute-done | bytes 69664 | tf_op jit(solution)/shard_map/ppermute | solution.py:226
  25.4 1.2 %collective-permute-start.13 = (bf16[256,128]{1,0:T(8,128)(2,1)S(1)}, bf16[256,128]{1,0:T(8,128)(2,1)S(1)}, u32[]{:S(2)}, u32[]{:S(2)}) collective-permute-start(bf16[256,128]{1,0:T(8,128)(2,1)S(1)} %shard_map.172.refs_8_), channel_id=1, source_target_pairs={{0,2},{1,3},{2,0},{3,1},{4,6},{5,7},{6,4},{7,5},{8,10},{9,11},{10,... | collective-permute-start | bytes 196616 | tf_op jit(solution)/shard_map/ppermute | solution.py:226
  26.6 0.0 collective-permute-done.6.refs_7_
  26.6 1.2 %collective-permute-start.2 = (bf16[136,256]{1,0:T(8,128)(2,1)S(1)}, bf16[136,256]{1,0:T(8,128)(2,1)S(1)}, u32[]{:S(2)}, u32[]{:S(2)}) collective-permute-start(bf16[136,256]{1,0:T(8,128)(2,1)S(1)} %collective-permute-done.1.refs_2_), channel_id=1, source_target_pairs={{0,4},{4,0},{8,12},{12,8},{16,20},{20,16},{24,28},{28,24},{1,5},{5... | collective-permute-start | bytes 208904 | tf_op jit(solution)/shard_map/ppermute | solution.py:226
  27.8 0.0 collective-permute-done.4.refs_5_
  27.8 0.0 collective-permute-start.12
  27.8 1.9 %collective-permute-done.13.refs_10_ = bf16[256,128]{1,0:T(8,128)(2,1)S(1)} collective-permute-done((bf16[256,128]{1,0:T(8,128)(2,1)S(1)}, bf16[256,128]{1,0:T(8,128)(2,1)S(1)}, u32[]{:S(2)}, u32[]{:S(2)}) %collective-permute-start.13) | collective-permute-done | bytes 65568 | tf_op jit(solution)/shard_map/ppermute | solution.py:226
  29.7 0.0 collective-permute-start.14
  29.7 1.3 %collective-permute-done.2.refs_3_ = bf16[136,256]{1,0:T(8,128)(2,1)S(1)} collective-permute-done((bf16[136,256]{1,0:T(8,128)(2,1)S(1)}, bf16[136,256]{1,0:T(8,128)(2,1)S(1)}, u32[]{:S(2)}, u32[]{:S(2)}) %collective-permute-start.2) | collective-permute-done | bytes 69664 | tf_op jit(solution)/shard_map/ppermute | solution.py:226
  30.9 0.0 collective-permute-done.9.refs_11_.refs_7_.refs_3_
  30.9 1.1 %shard_map.168 = (bf16[2,256,256]{2,1,0:T(8,128)(2,1)S(1)}, bf16[128,256]{1,0:T(8,128)(2,1)S(1)}, f32[2,2,256,256]{3,2,1,0:T(8,128)S(1)}) custom-call(s32[4,128]{1,0:T(4,128)S(1)} %get-tuple-element.23.place_ref, bf16[136,256]{1,0:T(8,128)(2,1)S(1)} %get-tuple-element.24.refs_0_.refs_3_, bf16[136,256]{1,0:T(8,128)(2,1)S(1)} %collective-permute-done.refs_1_, ...), custom_call_target="tpu_custom_call" | custom-call | flops 200000000 | bytes 2000000 | tf_op jit(solution)/shard_map/pallas_call | solution.py:292
  32.1 0.0 collective-permute-done.14.refs_11_
  32.1 1.1 %shard_map.173 = (bf16[128,256]{1,0:T(8,128)(2,1)S(1)}, bf16[32,128]{1,0:T(8,128)(2,1)S(1)}) custom-call(bf16[2,256,256]{2,1,0:T(8,128)(2,1)S(1)} %get-tuple-element.30.refs_0_, bf16[128,256]{1,0:T(8,128)(2,1)S(1)} %get-tuple-element.31.refs_1_, f32[2,2,256,256]{3,2,1,0:T(8,128)S(1)} %get-tuple-element.32.refs_2_, ...), custom_call_target="tpu_custom_call" | custom-call | flops 600000000 | bytes 3000000 | tf_op jit(solution)/shard_map/pallas_call | solution.py:292
  33.2 1.2 %collective-permute-start.18 = (bf16[32,128]{1,0:T(8,128)(2,1)S(1)}, bf16[32,128]{1,0:T(8,128)(2,1)S(1)}, u32[]{:S(2)}, u32[]{:S(2)}) collective-permute-start(bf16[32,128]{1,0:T(8,128)(2,1)S(1)} %get-tuple-element.43), channel_id=1, source_target_pairs={{0,4},{4,0},{8,12},{12,8},{16,20},{20,16},{24,28},{28,24},{1,5},{5... | collective-permute-start | bytes 24584 | tf_op jit(solution)/shard_map/ppermute | solution.py:226
  34.4 0.0 collective-permute-start.17
  34.4 0.9 %collective-permute-start.16 = (bf16[128,256]{1,0:T(8,128)(2,1)S(1)}, bf16[128,256]{1,0:T(8,128)(2,1)S(1)}, u32[]{:S(2)}, u32[]{:S(2)}) collective-permute-start(bf16[128,256]{1,0:T(8,128)(2,1)S(1)} %get-tuple-element.38.refs_0_), channel_id=1, source_target_pairs={{0,2},{1,3},{2,0},{3,1},{4,6},{5,7},{6,4},{7,5},{8,10},{9,11},{10,... | collective-permute-start | bytes 196616 | tf_op jit(solution)/shard_map/ppermute | solution.py:226
  35.3 1.0 %collective-permute-start.15 = (bf16[128,256]{1,0:T(8,128)(2,1)S(1)}, bf16[128,256]{1,0:T(8,128)(2,1)S(1)}, u32[]{:S(2)}, u32[]{:S(2)}) collective-permute-start(bf16[128,256]{1,0:T(8,128)(2,1)S(1)} %get-tuple-element.38.refs_0_), channel_id=1, source_target_pairs={{0,1},{1,0},{2,3},{3,2},{4,5},{5,4},{6,7},{7,6},{8,9},{9,8},{10,11... | collective-permute-start | bytes 196616 | tf_op jit(solution)/shard_map/ppermute | solution.py:226
  36.3 0.6 %collective-permute-done.18 = bf16[32,128]{1,0:T(8,128)(2,1)S(1)} collective-permute-done((bf16[32,128]{1,0:T(8,128)(2,1)S(1)}, bf16[32,128]{1,0:T(8,128)(2,1)S(1)}, u32[]{:S(2)}, u32[]{:S(2)}) %collective-permute-start.18) | collective-permute-done | bytes 8224 | tf_op jit(solution)/shard_map/ppermute | solution.py:226
  36.9 3.9 %collective-permute-start.21 = (bf16[2,32,128]{2,1,0:T(8,128)(2,1)S(1)}, bf16[2,32,128]{2,1,0:T(8,128)(2,1)S(1)}, u32[]{:S(2)}, u32[]{:S(2)}) collective-permute-start(bf16[2,32,128]{2,1,0:T(8,128)(2,1)S(1)} %pad_maximum_fusion.refs_0_), channel_id=1, source_target_pairs={{0,24},{4,28},{8,16},{12,20},{16,8},{20,12},{24,0},{28,4},{1,25},{... | collective-permute-start | bytes 49160 | tf_op jit(solution)/shard_map/ppermute | solution.py:226
  40.8 1.7 %collective-permute-done.21.refs_3_ = bf16[2,32,128]{2,1,0:T(8,128)(2,1)S(1)} collective-permute-done((bf16[2,32,128]{2,1,0:T(8,128)(2,1)S(1)}, bf16[2,32,128]{2,1,0:T(8,128)(2,1)S(1)}, u32[]{:S(2)}, u32[]{:S(2)}) %collective-permute-start.21) | collective-permute-done | bytes 16416 | tf_op jit(solution)/shard_map/ppermute | solution.py:226
  42.5 2.9 %collective-permute-done.20.refs_2_ = bf16[2,32,128]{2,1,0:T(8,128)(2,1)S(1)} collective-permute-done((bf16[2,32,128]{2,1,0:T(8,128)(2,1)S(1)}, bf16[2,32,128]{2,1,0:T(8,128)(2,1)S(1)}, u32[]{:S(2)}, u32[]{:S(2)}) %collective-permute-start.20) | collective-permute-done | bytes 16416 | tf_op jit(solution)/shard_map/ppermute | solution.py:226
  45.4 0.8 %collective-permute-done.19.refs_1_ = bf16[2,32,128]{2,1,0:T(8,128)(2,1)S(1)} collective-permute-done((bf16[2,32,128]{2,1,0:T(8,128)(2,1)S(1)}, bf16[2,32,128]{2,1,0:T(8,128)(2,1)S(1)}, u32[]{:S(2)}, u32[]{:S(2)}) %collective-permute-start.19) | collective-permute-done | bytes 16416 | tf_op jit(solution)/shard_map/ppermute | solution.py:226
  46.3 0.1 collective-permute-start.24
  46.4 1.6 %collective-permute-start.23 = (bf16[4,32,128]{2,1,0:T(8,128)(2,1)S(1)}, bf16[4,32,128]{2,1,0:T(8,128)(2,1)S(1)}, u32[]{:S(2)}, u32[]{:S(2)}) collective-permute-start(bf16[4,32,128]{2,1,0:T(8,128)(2,1)S(1)} %shard_map.176.refs_0_), channel_id=1, source_target_pairs={{0,2},{1,3},{2,0},{3,1},{4,6},{5,7},{6,4},{7,5},{8,10},{9,11},{10,... | collective-permute-start | bytes 98312 | tf_op jit(solution)/shard_map/ppermute | solution.py:226
  48.0 0.3 collective-permute-start.22
  48.2 0.4 shard_map.174.refs_6_
  48.7 1.9 %shard_map.175 = (bf16[1024,512]{1,0:T(8,128)(2,1)S(1)}, bf16[8,64,256]{2,1,0:T(8,128)(2,1)}) custom-call(bf16[128,256]{1,0:T(8,128)(2,1)S(1)} %get-tuple-element.38.refs_0_, bf16[128,256]{1,0:T(8,128)(2,1)S(1)} %collective-permute-done.15.refs_1_, bf16[128,256]{1,0:T(8,128)(2,1)S(1)} %collective-permute-done.16.refs_2_, ...), custom_call_target="tpu_custom_call" | custom-call | flops 300000000 | bytes 3000000 | tf_op jit(solution)/shard_map/pallas_call | solution.py:292
  50.7 1.6 %pair_update.1 = bf16[4,32,4096]{2,1,0:T(8,128)(2,1)} custom-call(f32[4,128]{1,0:T(4,128)S(1)} %get-tuple-element.29.refs_15_.open_ref, bf16[1024,512]{1,0:T(8,128)(2,1)S(1)} %get-tuple-element.41.table_ref, bf16[4,32,4096]{2,1,0:T(8,128)(2,1)S(1)} %get-tuple-element.34.pair_ref, f32[32,128]{1,0:T(8,128)S(1)} %get-tuple-element.42.offset_ref, ...), custom_call_target="tpu_custom_call" | custom-call | flops 600000000 | bytes 3000000 | tf_op jit(solution)/shard_map/pair_update/pallas_call | solution.py:979
  (14 shorter events, 0.1 us)
Async XLA Ops:
  2.7 3.5 %collective-permute-start.10 = (f32[2,8,5248]{2,1,0:T(8,128)S(1)}, f32[2,8,5248]{2,1,0:T(8,128)S(1)}, u32[]{:S(2)}, u32[]{:S(2)}) collective-permute-start(f32[2,8,5248]{2,1,0:T(8,128)S(1)} %shard_map.170), channel_id=1, source_target_pairs={{0,1},{1,0},{2,3},{3,2},{4,5},{5,4},{6,7},{7,6},{8,9},{9,8},{10,11... | collective-permute-start | bytes 1007624 | tf_op jit(solution)/shard_map/ppermute | solution.py:226
  3.3 9.7 %collective-permute-start.8 = (bf16[8,64,256]{2,1,0:T(8,128)(2,1)S(1)}, bf16[8,64,256]{2,1,0:T(8,128)(2,1)S(1)}, u32[]{:S(2)}, u32[]{:S(2)}) collective-permute-start(bf16[8,64,256]{2,1,0:T(8,128)(2,1)S(1)} %get-tuple-element.25.refs_8_.refs_4_.refs_0_), channel_id=1, source_target_pairs={{0,2},{1,3},{2,0},{3,1},{4,6},{5,7},{6,4},{7,5},{8,10},{9,11},{10,... | collective-permute-start | bytes 786440 | tf_op jit(solution)/shard_map/ppermute | solution.py:226
  6.4 16.0 %collective-permute-start.11 = (f32[8,5248]{1,0:T(8,128)S(1)}, f32[8,5248]{1,0:T(8,128)S(1)}, u32[]{:S(2)}, u32[]{:S(2)}) collective-permute-start(f32[8,5248]{1,0:T(8,128)S(1)} %get-tuple-element.36), channel_id=1, source_target_pairs={{0,2},{1,3},{2,0},{3,1},{4,6},{5,7},{6,4},{7,5},{8,10},{9,11},{10,... | collective-permute-start | bytes 503816 | tf_op jit(solution)/shard_map/ppermute | solution.py:226
  7.5 8.6 %collective-permute-start.5 = (bf16[136,256]{1,0:T(8,128)(2,1)S(1)}, bf16[136,256]{1,0:T(8,128)(2,1)S(1)}, u32[]{:S(2)}, u32[]{:S(2)}) collective-permute-start(bf16[136,256]{1,0:T(8,128)(2,1)S(1)} %get-tuple-element.24.refs_0_.refs_3_), channel_id=1, source_target_pairs={{0,24},{4,28},{8,16},{12,20},{16,8},{20,12},{24,0},{28,4},{1,25},{... | collective-permute-start | bytes 208904 | tf_op jit(solution)/shard_map/ppermute | solution.py:226
  11.2 19.8 %collective-permute-start.7 = (bf16[8,64,256]{2,1,0:T(8,128)(2,1)S(1)}, bf16[8,64,256]{2,1,0:T(8,128)(2,1)S(1)}, u32[]{:S(2)}, u32[]{:S(2)}) collective-permute-start(bf16[8,64,256]{2,1,0:T(8,128)(2,1)S(1)} %get-tuple-element.25.refs_8_.refs_4_.refs_0_), channel_id=1, source_target_pairs={{0,1},{1,0},{2,3},{3,2},{4,5},{5,4},{6,7},{7,6},{8,9},{9,8},{10,11... | collective-permute-start | bytes 786440 | tf_op jit(solution)/shard_map/ppermute | solution.py:226
  13.0 18.0 %collective-permute-start.9 = (bf16[8,64,256]{2,1,0:T(8,128)(2,1)S(1)}, bf16[8,64,256]{2,1,0:T(8,128)(2,1)S(1)}, u32[]{:S(2)}, u32[]{:S(2)}) collective-permute-start(bf16[8,64,256]{2,1,0:T(8,128)(2,1)S(1)} %collective-permute-done.8.refs_10_.refs_6_.refs_2_), channel_id=1, source_target_pairs={{0,1},{1,0},{2,3},{3,2},{4,5},{5,4},{6,7},{7,6},{8,9},{9,8},{10,11... | collective-permute-start | bytes 786440 | tf_op jit(solution)/shard_map/ppermute | solution.py:226
  13.0 7.4 %collective-permute-start.3 = (bf16[136,256]{1,0:T(8,128)(2,1)S(1)}, bf16[136,256]{1,0:T(8,128)(2,1)S(1)}, u32[]{:S(2)}, u32[]{:S(2)}) collective-permute-start(bf16[136,256]{1,0:T(8,128)(2,1)S(1)} %get-tuple-element.24.refs_0_.refs_3_), channel_id=1, source_target_pairs={{0,16},{4,20},{8,24},{12,28},{16,0},{20,4},{24,8},{28,12},{1,17},{... | collective-permute-start | bytes 208904 | tf_op jit(solution)/shard_map/ppermute | solution.py:226
  16.1 5.9 %collective-permute-start.1 = (bf16[136,256]{1,0:T(8,128)(2,1)S(1)}, bf16[136,256]{1,0:T(8,128)(2,1)S(1)}, u32[]{:S(2)}, u32[]{:S(2)}) collective-permute-start(bf16[136,256]{1,0:T(8,128)(2,1)S(1)} %get-tuple-element.24.refs_0_.refs_3_), channel_id=1, source_target_pairs={{0,8},{4,12},{8,0},{12,4},{16,24},{20,28},{24,16},{28,20},{1,9},{5... | collective-permute-start | bytes 208904 | tf_op jit(solution)/shard_map/ppermute | solution.py:226
  20.3 5.1 %collective-permute-start = (bf16[136,256]{1,0:T(8,128)(2,1)S(1)}, bf16[136,256]{1,0:T(8,128)(2,1)S(1)}, u32[]{:S(2)}, u32[]{:S(2)}) collective-permute-start(bf16[136,256]{1,0:T(8,128)(2,1)S(1)} %get-tuple-element.24.refs_0_.refs_3_), channel_id=1, source_target_pairs={{0,4},{4,0},{8,12},{12,8},{16,20},{20,16},{24,28},{28,24},{1,5},{5... | collective-permute-start | bytes 208904 | tf_op jit(solution)/shard_map/ppermute | solution.py:226
  22.0 4.6 %collective-permute-start.6 = (bf16[136,256]{1,0:T(8,128)(2,1)S(1)}, bf16[136,256]{1,0:T(8,128)(2,1)S(1)}, u32[]{:S(2)}, u32[]{:S(2)}) collective-permute-start(bf16[136,256]{1,0:T(8,128)(2,1)S(1)} %collective-permute-done.5.refs_6_), channel_id=1, source_target_pairs={{0,4},{4,0},{8,12},{12,8},{16,20},{20,16},{24,28},{28,24},{1,5},{5... | collective-permute-start | bytes 208904 | tf_op jit(solution)/shard_map/ppermute | solution.py:226
  22.4 5.4 %collective-permute-start.4 = (bf16[136,256]{1,0:T(8,128)(2,1)S(1)}, bf16[136,256]{1,0:T(8,128)(2,1)S(1)}, u32[]{:S(2)}, u32[]{:S(2)}) collective-permute-start(bf16[136,256]{1,0:T(8,128)(2,1)S(1)} %collective-permute-done.3.refs_4_), channel_id=1, source_target_pairs={{0,4},{4,0},{8,12},{12,8},{16,20},{20,16},{24,28},{28,24},{1,5},{5... | collective-permute-start | bytes 208904 | tf_op jit(solution)/shard_map/ppermute | solution.py:226
  25.4 4.3 %collective-permute-start.13 = (bf16[256,128]{1,0:T(8,128)(2,1)S(1)}, bf16[256,128]{1,0:T(8,128)(2,1)S(1)}, u32[]{:S(2)}, u32[]{:S(2)}) collective-permute-start(bf16[256,128]{1,0:T(8,128)(2,1)S(1)} %shard_map.172.refs_8_), channel_id=1, source_target_pairs={{0,2},{1,3},{2,0},{3,1},{4,6},{5,7},{6,4},{7,5},{8,10},{9,11},{10,... | collective-permute-start | bytes 196616 | tf_op jit(solution)/shard_map/ppermute | solution.py:226
  26.6 4.3 %collective-permute-start.2 = (bf16[136,256]{1,0:T(8,128)(2,1)S(1)}, bf16[136,256]{1,0:T(8,128)(2,1)S(1)}, u32[]{:S(2)}, u32[]{:S(2)}) collective-permute-start(bf16[136,256]{1,0:T(8,128)(2,1)S(1)} %collective-permute-done.1.refs_2_), channel_id=1, source_target_pairs={{0,4},{4,0},{8,12},{12,8},{16,20},{20,16},{24,28},{28,24},{1,5},{5... | collective-permute-start | bytes 208904 | tf_op jit(solution)/shard_map/ppermute | solution.py:226
  27.8 4.3 %collective-permute-start.12 = (bf16[256,128]{1,0:T(8,128)(2,1)S(1)}, bf16[256,128]{1,0:T(8,128)(2,1)S(1)}, u32[]{:S(2)}, u32[]{:S(2)}) collective-permute-start(bf16[256,128]{1,0:T(8,128)(2,1)S(1)} %shard_map.172.refs_8_), channel_id=1, source_target_pairs={{0,1},{1,0},{2,3},{3,2},{4,5},{5,4},{6,7},{7,6},{8,9},{9,8},{10,11... | collective-permute-start | bytes 196616 | tf_op jit(solution)/shard_map/ppermute | solution.py:226
  29.7 2.4 %collective-permute-start.14 = (bf16[256,128]{1,0:T(8,128)(2,1)S(1)}, bf16[256,128]{1,0:T(8,128)(2,1)S(1)}, u32[]{:S(2)}, u32[]{:S(2)}) collective-permute-start(bf16[256,128]{1,0:T(8,128)(2,1)S(1)} %collective-permute-done.13.refs_10_), channel_id=1, source_target_pairs={{0,1},{1,0},{2,3},{3,2},{4,5},{5,4},{6,7},{7,6},{8,9},{9,8},{10,11... | collective-permute-start | bytes 196616 | tf_op jit(solution)/shard_map/ppermute | solution.py:226
  33.2 3.7 %collective-permute-start.18 = (bf16[32,128]{1,0:T(8,128)(2,1)S(1)}, bf16[32,128]{1,0:T(8,128)(2,1)S(1)}, u32[]{:S(2)}, u32[]{:S(2)}) collective-permute-start(bf16[32,128]{1,0:T(8,128)(2,1)S(1)} %get-tuple-element.43), channel_id=1, source_target_pairs={{0,4},{4,0},{8,12},{12,8},{16,20},{20,16},{24,28},{28,24},{1,5},{5... | collective-permute-start | bytes 24584 | tf_op jit(solution)/shard_map/ppermute | solution.py:226
  34.4 13.6 %collective-permute-start.17 = (bf16[128,256]{1,0:T(8,128)(2,1)S(1)}, bf16[128,256]{1,0:T(8,128)(2,1)S(1)}, u32[]{:S(2)}, u32[]{:S(2)}) collective-permute-start(bf16[128,256]{1,0:T(8,128)(2,1)S(1)} %get-tuple-element.38.refs_0_), channel_id=1, source_target_pairs={{0,3},{1,2},{2,1},{3,0},{4,7},{5,6},{6,5},{7,4},{8,11},{9,10},{10,... | collective-permute-start | bytes 196616 | tf_op jit(solution)/shard_map/ppermute | solution.py:226
  34.4 14.3 %collective-permute-start.16 = (bf16[128,256]{1,0:T(8,128)(2,1)S(1)}, bf16[128,256]{1,0:T(8,128)(2,1)S(1)}, u32[]{:S(2)}, u32[]{:S(2)}) collective-permute-start(bf16[128,256]{1,0:T(8,128)(2,1)S(1)} %get-tuple-element.38.refs_0_), channel_id=1, source_target_pairs={{0,2},{1,3},{2,0},{3,1},{4,6},{5,7},{6,4},{7,5},{8,10},{9,11},{10,... | collective-permute-start | bytes 196616 | tf_op jit(solution)/shard_map/ppermute | solution.py:226
  35.3 13.4 %collective-permute-start.15 = (bf16[128,256]{1,0:T(8,128)(2,1)S(1)}, bf16[128,256]{1,0:T(8,128)(2,1)S(1)}, u32[]{:S(2)}, u32[]{:S(2)}) collective-permute-start(bf16[128,256]{1,0:T(8,128)(2,1)S(1)} %get-tuple-element.38.refs_0_), channel_id=1, source_target_pairs={{0,1},{1,0},{2,3},{3,2},{4,5},{5,4},{6,7},{7,6},{8,9},{9,8},{10,11... | collective-permute-start | bytes 196616 | tf_op jit(solution)/shard_map/ppermute | solution.py:226
  36.9 5.6 %collective-permute-start.21 = (bf16[2,32,128]{2,1,0:T(8,128)(2,1)S(1)}, bf16[2,32,128]{2,1,0:T(8,128)(2,1)S(1)}, u32[]{:S(2)}, u32[]{:S(2)}) collective-permute-start(bf16[2,32,128]{2,1,0:T(8,128)(2,1)S(1)} %pad_maximum_fusion.refs_0_), channel_id=1, source_target_pairs={{0,24},{4,28},{8,16},{12,20},{16,8},{20,12},{24,0},{28,4},{1,25},{... | collective-permute-start | bytes 49160 | tf_op jit(solution)/shard_map/ppermute | solution.py:226
  40.8 4.6 %collective-permute-start.20 = (bf16[2,32,128]{2,1,0:T(8,128)(2,1)S(1)}, bf16[2,32,128]{2,1,0:T(8,128)(2,1)S(1)}, u32[]{:S(2)}, u32[]{:S(2)}) collective-permute-start(bf16[2,32,128]{2,1,0:T(8,128)(2,1)S(1)} %pad_maximum_fusion.refs_0_), channel_id=1, source_target_pairs={{0,16},{4,20},{8,24},{12,28},{16,0},{20,4},{24,8},{28,12},{1,17},{... | collective-permute-start | bytes 49160 | tf_op jit(solution)/shard_map/ppermute | solution.py:226
  42.5 3.7 %collective-permute-start.19 = (bf16[2,32,128]{2,1,0:T(8,128)(2,1)S(1)}, bf16[2,32,128]{2,1,0:T(8,128)(2,1)S(1)}, u32[]{:S(2)}, u32[]{:S(2)}) collective-permute-start(bf16[2,32,128]{2,1,0:T(8,128)(2,1)S(1)} %pad_maximum_fusion.refs_0_), channel_id=1, source_target_pairs={{0,8},{4,12},{8,0},{12,4},{16,24},{20,28},{24,16},{28,20},{1,9},{5... | collective-permute-start | bytes 49160 | tf_op jit(solution)/shard_map/ppermute | solution.py:226
  46.3 4.3 %collective-permute-start.24 = (bf16[4,32,128]{2,1,0:T(8,128)(2,1)S(1)}, bf16[4,32,128]{2,1,0:T(8,128)(2,1)S(1)}, u32[]{:S(2)}, u32[]{:S(2)}) collective-permute-start(bf16[4,32,128]{2,1,0:T(8,128)(2,1)S(1)} %shard_map.176.refs_0_), channel_id=1, source_target_pairs={{0,3},{1,2},{2,1},{3,0},{4,7},{5,6},{6,5},{7,4},{8,11},{9,10},{10,... | collective-permute-start | bytes 98312 | tf_op jit(solution)/shard_map/ppermute | solution.py:226
  46.4 4.3 %collective-permute-start.23 = (bf16[4,32,128]{2,1,0:T(8,128)(2,1)S(1)}, bf16[4,32,128]{2,1,0:T(8,128)(2,1)S(1)}, u32[]{:S(2)}, u32[]{:S(2)}) collective-permute-start(bf16[4,32,128]{2,1,0:T(8,128)(2,1)S(1)} %shard_map.176.refs_0_), channel_id=1, source_target_pairs={{0,2},{1,3},{2,0},{3,1},{4,6},{5,7},{6,4},{7,5},{8,10},{9,11},{10,... | collective-permute-start | bytes 98312 | tf_op jit(solution)/shard_map/ppermute | solution.py:226
  48.0 2.7 %collective-permute-start.22 = (bf16[4,32,128]{2,1,0:T(8,128)(2,1)S(1)}, bf16[4,32,128]{2,1,0:T(8,128)(2,1)S(1)}, u32[]{:S(2)}, u32[]{:S(2)}) collective-permute-start(bf16[4,32,128]{2,1,0:T(8,128)(2,1)S(1)} %shard_map.176.refs_0_), channel_id=1, source_target_pairs={{0,1},{1,0},{2,3},{3,2},{4,5},{5,4},{6,7},{7,6},{8,9},{9,8},{10,11... | collective-permute-start | bytes 98312 | tf_op jit(solution)/shard_map/ppermute | solution.py:226
